TPU v7x, 512 devices: a whole 4x8x8 slice. The times are simulated.
512 devices in a mesh: tm: 256 (over z, y, x), state: 2 (over core).
Axes of the slice: x: 4, y: 8, z: 8, core: 2. Of those that a mesh axis runs over, the one named last changes fastest.
Arguments:
- features: float32 [4, 4096, 512], P(None, 'tm'), may hold values from -18 to 18
- gauss_means: float32 [1024, 512], P('state'), may hold values from -3 to 3
- precisions: float32 [1024, 512], P('state'), may hold values from 0.5 to 2
- transitions: bfloat16 [1024, 1024], P('state'), may hold values from 0 to 1, as said below
- initial: bfloat16 [1024], P('state'), may hold values from 0.099609375 to 10
- reset_flags: int32 [4, 4096], P(None, 'tm'), may hold values from 0 to 1, as said below
Outputs:
- posteriors: bfloat16 [4, 4096, 1024], P(None, 'tm', 'state')
- evidence: float32 [4, 4096], P(None, ('tm', 'state'))
Inputs may be any that keep to these rules, and one draw needn't show every extreme that they name: `transitions`: every entry nonnegative; each row sums to 1 up to the rounding of its entries; the diagonal holds half or more of each row. reset_flags[b, 0] = 1 in every stream; the runs of frames from one 1 to the next (utterances) hold 1 to 16 frames, and some hold exactly 16.
All inputs are finite; a program needn't handle non-finite values.
Results may differ from a plain program's by a relative error of at most 0.012.
Values may be sent and summed in bfloat16 or wider, within the bound.
No kernel may reach another device: no remote copies, remote signals or barrier semaphores. Data moves between devices by JAX's collectives and lax.ppermute only.
A program may use at most 64 MiB of HBM per device.

v0:
```python
import jax
import jax.numpy as jnp
from jax import lax
from jax.sharding import PartitionSpec as P

SPAN = 1


acoustic = 0.1


def in_one_piece(arrays, axis, dim, along):
    columns = [a.reshape(*a.shape[:along], -1) for a in arrays]
    both = jnp.concatenate(columns, axis=along)
    out, at, gathered = (lax.all_gather(both, axis, axis=dim, tiled=True), 0, [])
    for a, column in zip(arrays, columns):
        piece = out[..., at : at + column.shape[along]]
        gathered.append(piece.reshape(*piece.shape[:along], *a.shape[along:]))
        at += column.shape[along]
    return tuple(gathered)


def passed_along(block, axis, distance):
    devices = range(lax.axis_size(axis))
    route = [(i - distance, i) for i in devices if i - distance in devices]
    return lax.ppermute(block, axis, route)


def local_scores(features, gauss_means, precisions):
    streams, frames, feat_width = features.shape
    highest = lax.Precision.HIGHEST
    flat_feats = features.reshape(streams * frames, feat_width)
    quadratic = jnp.dot(flat_feats * flat_feats, (-0.5 * precisions).T, precision=highest)
    linear_part = jnp.dot(flat_feats, (precisions * gauss_means).T, precision=highest)
    offset = 0.5 * jnp.sum(jnp.log(precisions) - precisions * gauss_means * gauss_means, axis=1)
    return (acoustic * (quadratic + linear_part + offset)).reshape(
        streams, frames, gauss_means.shape[0]
    )


def run_block(emission_t, reset_t, trans, trans_back, prior_dist, alpha_in, beta_in):
    states = trans.shape[0]

    def forward_step(alpha_prev, inputs):
        emit_row, reset_row = inputs
        predicted = jnp.dot(
            alpha_prev.astype(jnp.bfloat16), trans, preferred_element_type=jnp.float32
        )
        predicted = jnp.where(reset_row[:, None] == 1, prior_dist[None, :], predicted)
        weighted = emit_row * predicted
        norm_total = jnp.sum(weighted, axis=1)
        alpha_next = weighted / norm_total[:, None]
        return (alpha_next, (alpha_next, jnp.log(norm_total)))

    alpha_out, (alphas, log_norms) = lax.scan(forward_step, alpha_in, (emission_t, reset_t))

    def backward_step(beta_next, inputs):
        emit_row, reset_row = inputs
        spread = jnp.dot(
            (emit_row * beta_next).astype(jnp.bfloat16),
            trans_back,
            preferred_element_type=jnp.float32,
        )
        spread = spread / jnp.sum(spread, axis=1, keepdims=True)
        beta_prev = jnp.where(reset_row[:, None] == 1, 1.0 / states, spread)
        return (beta_prev, beta_next)

    beta_out, betas = lax.scan(backward_step, beta_in, (emission_t, reset_t), reverse=True)
    return (alpha_out, alphas, log_norms, beta_out, betas)


def run_chain(scores, resets, trans, trans_back, prior_dist, relay_step, relays):
    maxima = jnp.max(scores, axis=2, keepdims=True)
    emission_t = jnp.swapaxes(jnp.exp(scores - maxima), 0, 1)
    reset_t = jnp.swapaxes(resets, 0, 1)
    streams, states = (scores.shape[0], scores.shape[2])
    alpha_in = jnp.full((streams, states), 1.0 / states, jnp.float32)
    beta_in = alpha_in
    for relay_turn in range(relays + 1):
        alpha_out, alphas, log_norms, beta_out, betas = run_block(
            emission_t, reset_t, trans, trans_back, prior_dist, alpha_in, beta_in
        )
        if relay_turn < relays:
            alpha_in, beta_in = relay_step(alpha_out, beta_out)
    product = alphas * betas
    posterior = (product / jnp.sum(product, axis=2, keepdims=True)).astype(jnp.bfloat16)
    return (jnp.swapaxes(posterior, 0, 1), jnp.swapaxes(log_norms, 0, 1))


def per_device(features, gauss_means, precisions, transitions, initial, reset_flags):
    trans, prior_raw = in_one_piece((transitions, initial), "state", 0, 1)
    trans_back = trans.T
    states = trans.shape[0]
    prior_float = prior_raw.astype(jnp.float32)
    prior_dist = prior_float / jnp.sum(prior_float)
    scores = local_scores(features, gauss_means, precisions)
    group = lax.axis_size("state")
    place = lax.axis_index("state")
    blocks = lax.axis_size("tm")
    block_place = lax.axis_index("tm")
    quarter = features.shape[1] // group
    is_last = block_place * group + place == blocks * group - 1

    def relay_step(alpha_out, beta_out):
        alpha_next = passed_along(alpha_out, ("tm", "state"), 1)
        beta_next = passed_along(beta_out, ("tm", "state"), -1)
        beta_next = jnp.where(is_last, 1.0 / states, beta_next)
        return (alpha_next, beta_next)

    my_scores = lax.all_to_all(scores, "state", split_axis=1, concat_axis=2, tiled=True)
    my_flags = lax.dynamic_slice_in_dim(reset_flags, place * quarter, quarter, 1)
    posterior, evidence = run_chain(
        my_scores, my_flags, trans, trans_back, prior_dist, relay_step, SPAN * group
    )
    posteriors = lax.all_to_all(posterior, "state", split_axis=2, concat_axis=1, tiled=True)
    return (posteriors, evidence)


def solution(mesh):
    return jax.shard_map(
        per_device,
        mesh=mesh,
        in_specs=(
            P(None, "tm", None),
            P("state", None),
            P("state", None),
            P("state", None),
            P("state"),
            P(None, "tm"),
        ),
        out_specs=(P(None, "tm", "state"), P(None, ("tm", "state"))),
        check_vma=False,
    )
```

profile of v0, /device:TPU:257, one launch (start us, length us, event | category | flops | bytes accessed | tf_op | source)
XLA Modules:
  0.0 149.7 jit_solution(1743918318548357542)
XLA Ops:
  7.2 1.5 %copy.41 = bf16[512,1024]{0,1:T(8,128)(2,1)S(1)} copy(bf16[512,1024]{1,0:T(8,128)(2,1)} %param.21) | data formatting | bytes 2097152 | tf_op args[3]
  8.8 1.1 pad_maximum_fusion
  11.0 1.1 fusion.30
  12.0 1.2 fusion.27
  14.0 4.0 %all-to-all-start = ((f32[4,16,512]{2,0,1:T(4,128)}), f32[4,16,512]{2,0,1:T(4,128)S(1)}, u32[]{:S(2)}, u32[]{:S(2)}) async-start(f32[4,16,512]{2,0,1:T(4,128)} %copy.38), calls=%async_computation | async-start | bytes 262144 | tf_op jit(solution)/shard_map/all_to_all | solution.py:110
  19.4 11.7 %all-gather.2.cloned.1.call-done = bf16[1024,1025]{0,1:T(8,128)(2,1)} async-done(((bf16[512,1025]{0,1:T(8,128)(2,1)}), bf16[1024,1025]{0,1:T(8,128)(2,1)}) %all-gather.2.cloned.1.call-update) | async-done | bytes 2099216 | tf_op jit(solution)/shard_map/all_gather | solution.py:15
  31.1 3.5 %slice_bitcast_fusion = (bf16[1024,1024]{1,0:T(8,128)(2,1)S(1)}, bf16[1024,1024]{0,1:T(8,128)(2,1)}) fusion(bf16[1024,1025]{0,1:T(8,128)(2,1)} %all-gather.2.cloned.1.call-done), kind=kLoop, calls=%fused_computation.68 | loop fusion | bytes 6291456 | tf_op jit(solution)/shard_map/transpose | solution.py:92
  34.6 3.9 %copy.42 = bf16[1024,1024]{1,0:T(8,128)(2,1)} copy(bf16[1024,1024]{0,1:T(8,128)(2,1)} %get-tuple-element.648) | data formatting | bytes 4194304
  38.5 1.4 fusion.37
  39.9 1.3 fusion.36
  41.2 17.6 %while.84 = (s32[]{:T(128)}, f32[4,1024]{1,0:T(4,128)S(1)}, f32[8,4,1024]{2,1,0:T(4,128)S(1)}, s32[8,4]{1,0:T(8,128)S(1)}, f32[1024]{0:T(1024)S(1)}, /*index=5*/bf16[1024,1024]{1,0:T(8,128)(2,1)}, s32[]{:T(128)}, s32[]{:T(128)}) while((s32[]{:T(128)}, f32[4,1024]{1,0:T(4,128)S(1)}, f32[8,4,1024]{2,1,0:T(4,128)S(1)}, ...), condition=%wide.region_5.6_spmd.clone, body=%wide.region_3.5_spmd.clone.sunk | while | flops 8409091 | bytes 2183327 | solution.py:55
  41.2 2.1 %fusion.76 = (f32[4]{0:T(128)S(1)}, f32[4,1024]{1,0:T(4,128)S(1)}) fusion(bf16[1024,1024]{1,0:T(8,128)(2,1)} %get-tuple-element.916, f32[4,1024]{1,0:T(4,128)S(1)} %get-tuple-element.904, pred[]{:T(512)S(6)} %compare.6, f32[1024]{0:T(1024)S(1)} %get-tuple-element.915, pred[4]{0:T(512)(128)(4,1)S(1)} %compare_bitcast_fusion.16, ...), kind=kOutput, calls=%fused_computation.73.clone.1 | convolution fusion | flops 8404988 | bytes 2150425 | tf_op jit(solution)/shard_map/while/body/eval_jaxpr/dot_general | solution.py:46
  43.4 2.1 %fusion.76 = (f32[4]{0:T(128)S(1)}, f32[4,1024]{1,0:T(4,128)S(1)}) fusion(bf16[1024,1024]{1,0:T(8,128)(2,1)} %get-tuple-element.916, f32[4,1024]{1,0:T(4,128)S(1)} %get-tuple-element.904, pred[]{:T(512)S(6)} %compare.6, f32[1024]{0:T(1024)S(1)} %get-tuple-element.915, pred[4]{0:T(512)(128)(4,1)S(1)} %compare_bitcast_fusion.16, ...), kind=kOutput, calls=%fused_computation.73.clone.1 | convolution fusion | flops 8404988 | bytes 2150425 | tf_op jit(solution)/shard_map/while/body/eval_jaxpr/dot_general | solution.py:46
  45.6 2.1 %fusion.76 = (f32[4]{0:T(128)S(1)}, f32[4,1024]{1,0:T(4,128)S(1)}) fusion(bf16[1024,1024]{1,0:T(8,128)(2,1)} %get-tuple-element.916, f32[4,1024]{1,0:T(4,128)S(1)} %get-tuple-element.904, pred[]{:T(512)S(6)} %compare.6, f32[1024]{0:T(1024)S(1)} %get-tuple-element.915, pred[4]{0:T(512)(128)(4,1)S(1)} %compare_bitcast_fusion.16, ...), kind=kOutput, calls=%fused_computation.73.clone.1 | convolution fusion | flops 8404988 | bytes 2150425 | tf_op jit(solution)/shard_map/while/body/eval_jaxpr/dot_general | solution.py:46
  47.8 2.1 %fusion.76 = (f32[4]{0:T(128)S(1)}, f32[4,1024]{1,0:T(4,128)S(1)}) fusion(bf16[1024,1024]{1,0:T(8,128)(2,1)} %get-tuple-element.916, f32[4,1024]{1,0:T(4,128)S(1)} %get-tuple-element.904, pred[]{:T(512)S(6)} %compare.6, f32[1024]{0:T(1024)S(1)} %get-tuple-element.915, pred[4]{0:T(512)(128)(4,1)S(1)} %compare_bitcast_fusion.16, ...), kind=kOutput, calls=%fused_computation.73.clone.1 | convolution fusion | flops 8404988 | bytes 2150425 | tf_op jit(solution)/shard_map/while/body/eval_jaxpr/dot_general | solution.py:46
  50.0 2.1 %fusion.76 = (f32[4]{0:T(128)S(1)}, f32[4,1024]{1,0:T(4,128)S(1)}) fusion(bf16[1024,1024]{1,0:T(8,128)(2,1)} %get-tuple-element.916, f32[4,1024]{1,0:T(4,128)S(1)} %get-tuple-element.904, pred[]{:T(512)S(6)} %compare.6, f32[1024]{0:T(1024)S(1)} %get-tuple-element.915, pred[4]{0:T(512)(128)(4,1)S(1)} %compare_bitcast_fusion.16, ...), kind=kOutput, calls=%fused_computation.73.clone.1 | convolution fusion | flops 8404988 | bytes 2150425 | tf_op jit(solution)/shard_map/while/body/eval_jaxpr/dot_general | solution.py:46
  52.2 2.1 %fusion.76 = (f32[4]{0:T(128)S(1)}, f32[4,1024]{1,0:T(4,128)S(1)}) fusion(bf16[1024,1024]{1,0:T(8,128)(2,1)} %get-tuple-element.916, f32[4,1024]{1,0:T(4,128)S(1)} %get-tuple-element.904, pred[]{:T(512)S(6)} %compare.6, f32[1024]{0:T(1024)S(1)} %get-tuple-element.915, pred[4]{0:T(512)(128)(4,1)S(1)} %compare_bitcast_fusion.16, ...), kind=kOutput, calls=%fused_computation.73.clone.1 | convolution fusion | flops 8404988 | bytes 2150425 | tf_op jit(solution)/shard_map/while/body/eval_jaxpr/dot_general | solution.py:46
  54.4 2.1 %fusion.76 = (f32[4]{0:T(128)S(1)}, f32[4,1024]{1,0:T(4,128)S(1)}) fusion(bf16[1024,1024]{1,0:T(8,128)(2,1)} %get-tuple-element.916, f32[4,1024]{1,0:T(4,128)S(1)} %get-tuple-element.904, pred[]{:T(512)S(6)} %compare.6, f32[1024]{0:T(1024)S(1)} %get-tuple-element.915, pred[4]{0:T(512)(128)(4,1)S(1)} %compare_bitcast_fusion.16, ...), kind=kOutput, calls=%fused_computation.73.clone.1 | convolution fusion | flops 8404988 | bytes 2150425 | tf_op jit(solution)/shard_map/while/body/eval_jaxpr/dot_general | solution.py:46
  56.6 2.1 %fusion.76 = (f32[4]{0:T(128)S(1)}, f32[4,1024]{1,0:T(4,128)S(1)}) fusion(bf16[1024,1024]{1,0:T(8,128)(2,1)} %get-tuple-element.916, f32[4,1024]{1,0:T(4,128)S(1)} %get-tuple-element.904, pred[]{:T(512)S(6)} %compare.6, f32[1024]{0:T(1024)S(1)} %get-tuple-element.915, pred[4]{0:T(512)(128)(4,1)S(1)} %compare_bitcast_fusion.16, ...), kind=kOutput, calls=%fused_computation.73.clone.1 | convolution fusion | flops 8404988 | bytes 2150425 | tf_op jit(solution)/shard_map/while/body/eval_jaxpr/dot_general | solution.py:46
  58.8 3.2 %collective-permute-start = (f32[4,1024]{1,0:T(4,128)S(1)}, f32[4,1024]{1,0:T(4,128)S(1)}, u32[]{:S(2)}, u32[]{:S(2)}) collective-permute-start(f32[4,1024]{1,0:T(4,128)S(1)} %get-tuple-element.437), channel_id=1, source_target_pairs={{0,1},{1,2},{2,3},{3,4},{4,5},{5,6},{6,7},{7,8},{8,9},{9,10},{10,1... | collective-permute-start | bytes 49160 | tf_op jit(solution)/shard_map/ppermute | solution.py:26
  62.0 4.8 %while.85 = (s32[]{:T(128)}, f32[4,1024]{1,0:T(4,128)S(1)}, s32[8,4]{1,0:T(8,128)S(1)}, f32[8,4,1024]{2,1,0:T(4,128)S(1)}, bf16[1024,1024]{1,0:T(8,128)(2,1)S(1)}, /*index=5*/s32[]{:T(128)}, s32[]{:T(128)}, s32[]{:T(128)}) while((s32[]{:T(128)}, f32[4,1024]{1,0:T(4,128)S(1)}, s32[8,4]{1,0:T(8,128)S(1)}, ...), condition=%wide.region_14.15_spmd.clone, body=%wide.region_12.14_spmd.clone.sunk | while | flops 8413188 | bytes 2179243 | solution.py:68
  66.8 1.9 %collective-permute-start.2 = (f32[4,1024]{1,0:T(4,128)S(1)}, f32[4,1024]{1,0:T(4,128)S(1)}, u32[]{:S(2)}, u32[]{:S(2)}) collective-permute-start(f32[4,1024]{1,0:T(4,128)S(1)} %get-tuple-element.440), channel_id=1, source_target_pairs={{1,0},{2,1},{3,2},{4,3},{5,4},{6,5},{7,6},{8,7},{9,8},{10,9},{11,1... | collective-permute-start | bytes 49160 | tf_op jit(solution)/shard_map/ppermute | solution.py:26
  68.7 17.6 %while.80 = (s32[]{:T(128)}, f32[4,1024]{1,0:T(4,128)S(1)}, f32[8,4,1024]{2,1,0:T(4,128)S(1)}, s32[8,4]{1,0:T(8,128)S(1)}, f32[1024]{0:T(1024)S(1)}, /*index=5*/bf16[1024,1024]{1,0:T(8,128)(2,1)}, s32[]{:T(128)}) while((s32[]{:T(128)}, f32[4,1024]{1,0:T(4,128)S(1)}, f32[8,4,1024]{2,1,0:T(4,128)S(1)}, s32[8,4]{1,0:T(8,128)S(1)}, ...), condition=%wide.region_8.9_spmd, body=%wide.region_6.8_spmd.sunk | while | flops 8409090 | bytes 2183309 | solution.py:55
  68.7 2.1 %fusion.67 = (f32[4]{0:T(128)S(1)}, f32[4,1024]{1,0:T(4,128)S(1)}) fusion(bf16[1024,1024]{1,0:T(8,128)(2,1)} %get-tuple-element.938, f32[4,1024]{1,0:T(4,128)S(1)} %get-tuple-element.927, f32[1024]{0:T(1024)S(1)} %get-tuple-element.937, pred[4]{0:T(512)(128)(4,1)S(1)} %compare_bitcast_fusion.12, f32[8,4,1024]{2,1,0:T(4,128)S(1)} %get-tuple-element.935, ...), kind=kOutput, calls=%fused_computation.69.clone.1 | convolution fusion | flops 8404988 | bytes 2150424 | tf_op jit(solution)/shard_map/while/body/eval_jaxpr/dot_general | solution.py:46
  70.9 2.1 %fusion.67 = (f32[4]{0:T(128)S(1)}, f32[4,1024]{1,0:T(4,128)S(1)}) fusion(bf16[1024,1024]{1,0:T(8,128)(2,1)} %get-tuple-element.938, f32[4,1024]{1,0:T(4,128)S(1)} %get-tuple-element.927, f32[1024]{0:T(1024)S(1)} %get-tuple-element.937, pred[4]{0:T(512)(128)(4,1)S(1)} %compare_bitcast_fusion.12, f32[8,4,1024]{2,1,0:T(4,128)S(1)} %get-tuple-element.935, ...), kind=kOutput, calls=%fused_computation.69.clone.1 | convolution fusion | flops 8404988 | bytes 2150424 | tf_op jit(solution)/shard_map/while/body/eval_jaxpr/dot_general | solution.py:46
  73.1 2.1 %fusion.67 = (f32[4]{0:T(128)S(1)}, f32[4,1024]{1,0:T(4,128)S(1)}) fusion(bf16[1024,1024]{1,0:T(8,128)(2,1)} %get-tuple-element.938, f32[4,1024]{1,0:T(4,128)S(1)} %get-tuple-element.927, f32[1024]{0:T(1024)S(1)} %get-tuple-element.937, pred[4]{0:T(512)(128)(4,1)S(1)} %compare_bitcast_fusion.12, f32[8,4,1024]{2,1,0:T(4,128)S(1)} %get-tuple-element.935, ...), kind=kOutput, calls=%fused_computation.69.clone.1 | convolution fusion | flops 8404988 | bytes 2150424 | tf_op jit(solution)/shard_map/while/body/eval_jaxpr/dot_general | solution.py:46
  75.3 2.1 %fusion.67 = (f32[4]{0:T(128)S(1)}, f32[4,1024]{1,0:T(4,128)S(1)}) fusion(bf16[1024,1024]{1,0:T(8,128)(2,1)} %get-tuple-element.938, f32[4,1024]{1,0:T(4,128)S(1)} %get-tuple-element.927, f32[1024]{0:T(1024)S(1)} %get-tuple-element.937, pred[4]{0:T(512)(128)(4,1)S(1)} %compare_bitcast_fusion.12, f32[8,4,1024]{2,1,0:T(4,128)S(1)} %get-tuple-element.935, ...), kind=kOutput, calls=%fused_computation.69.clone.1 | convolution fusion | flops 8404988 | bytes 2150424 | tf_op jit(solution)/shard_map/while/body/eval_jaxpr/dot_general | solution.py:46
  77.5 2.1 %fusion.67 = (f32[4]{0:T(128)S(1)}, f32[4,1024]{1,0:T(4,128)S(1)}) fusion(bf16[1024,1024]{1,0:T(8,128)(2,1)} %get-tuple-element.938, f32[4,1024]{1,0:T(4,128)S(1)} %get-tuple-element.927, f32[1024]{0:T(1024)S(1)} %get-tuple-element.937, pred[4]{0:T(512)(128)(4,1)S(1)} %compare_bitcast_fusion.12, f32[8,4,1024]{2,1,0:T(4,128)S(1)} %get-tuple-element.935, ...), kind=kOutput, calls=%fused_computation.69.clone.1 | convolution fusion | flops 8404988 | bytes 2150424 | tf_op jit(solution)/shard_map/while/body/eval_jaxpr/dot_general | solution.py:46
  79.7 2.1 %fusion.67 = (f32[4]{0:T(128)S(1)}, f32[4,1024]{1,0:T(4,128)S(1)}) fusion(bf16[1024,1024]{1,0:T(8,128)(2,1)} %get-tuple-element.938, f32[4,1024]{1,0:T(4,128)S(1)} %get-tuple-element.927, f32[1024]{0:T(1024)S(1)} %get-tuple-element.937, pred[4]{0:T(512)(128)(4,1)S(1)} %compare_bitcast_fusion.12, f32[8,4,1024]{2,1,0:T(4,128)S(1)} %get-tuple-element.935, ...), kind=kOutput, calls=%fused_computation.69.clone.1 | convolution fusion | flops 8404988 | bytes 2150424 | tf_op jit(solution)/shard_map/while/body/eval_jaxpr/dot_general | solution.py:46
  81.9 2.1 %fusion.67 = (f32[4]{0:T(128)S(1)}, f32[4,1024]{1,0:T(4,128)S(1)}) fusion(bf16[1024,1024]{1,0:T(8,128)(2,1)} %get-tuple-element.938, f32[4,1024]{1,0:T(4,128)S(1)} %get-tuple-element.927, f32[1024]{0:T(1024)S(1)} %get-tuple-element.937, pred[4]{0:T(512)(128)(4,1)S(1)} %compare_bitcast_fusion.12, f32[8,4,1024]{2,1,0:T(4,128)S(1)} %get-tuple-element.935, ...), kind=kOutput, calls=%fused_computation.69.clone.1 | convolution fusion | flops 8404988 | bytes 2150424 | tf_op jit(solution)/shard_map/while/body/eval_jaxpr/dot_general | solution.py:46
  84.1 2.1 %fusion.67 = (f32[4]{0:T(128)S(1)}, f32[4,1024]{1,0:T(4,128)S(1)}) fusion(bf16[1024,1024]{1,0:T(8,128)(2,1)} %get-tuple-element.938, f32[4,1024]{1,0:T(4,128)S(1)} %get-tuple-element.927, f32[1024]{0:T(1024)S(1)} %get-tuple-element.937, pred[4]{0:T(512)(128)(4,1)S(1)} %compare_bitcast_fusion.12, f32[8,4,1024]{2,1,0:T(4,128)S(1)} %get-tuple-element.935, ...), kind=kOutput, calls=%fused_computation.69.clone.1 | convolution fusion | flops 8404988 | bytes 2150424 | tf_op jit(solution)/shard_map/while/body/eval_jaxpr/dot_general | solution.py:46
  86.3 3.6 %collective-permute-start.1 = (f32[4,1024]{1,0:T(4,128)S(1)}, f32[4,1024]{1,0:T(4,128)S(1)}, u32[]{:S(2)}, u32[]{:S(2)}) collective-permute-start(f32[4,1024]{1,0:T(4,128)S(1)} %get-tuple-element.438), channel_id=1, source_target_pairs={{0,1},{1,2},{2,3},{3,4},{4,5},{5,6},{6,7},{7,8},{8,9},{9,10},{10,1... | collective-permute-start | bytes 49160 | tf_op jit(solution)/shard_map/ppermute | solution.py:26
  90.0 4.8 %while.82 = (s32[]{:T(128)}, f32[4,1024]{1,0:T(4,128)S(1)}, s32[8,4]{1,0:T(8,128)S(1)}, f32[8,4,1024]{2,1,0:T(4,128)S(1)}, bf16[1024,1024]{1,0:T(8,128)(2,1)S(1)}, /*index=5*/s32[]{:T(128)}, s32[]{:T(128)}) while((s32[]{:T(128)}, f32[4,1024]{1,0:T(4,128)S(1)}, s32[8,4]{1,0:T(8,128)S(1)}, f32[8,4,1024]{2,1,0:T(4,128)S(1)}, ...), condition=%wide.region_17.18_spmd, body=%wide.region_15.17_spmd.sunk | while | flops 8409091 | bytes 2179225 | solution.py:68
  94.7 6.3 %collective-permute-start.3 = (f32[4,1024]{1,0:T(4,128)S(1)}, f32[4,1024]{1,0:T(4,128)S(1)}, u32[]{:S(2)}, u32[]{:S(2)}) collective-permute-start(f32[4,1024]{1,0:T(4,128)S(1)} %get-tuple-element.441), channel_id=1, source_target_pairs={{1,0},{2,1},{3,2},{4,3},{5,4},{6,5},{7,6},{8,7},{9,8},{10,9},{11,1... | collective-permute-start | bytes 49160 | tf_op jit(solution)/shard_map/ppermute | solution.py:26
  101.0 20.0 %while.81 = (s32[]{:T(128)}, f32[4,1024]{1,0:T(4,128)S(1)}, f32[8,4,1024]{2,0,1:T(8,128)S(1)}, f32[8,4]{1,0:T(8,128)S(1)}, f32[8,4,1024]{2,1,0:T(4,128)S(1)}, /*...) while((s32[]{:T(128)}, f32[4,1024]{1,0:T(4,128)S(1)}, ...), condition=%wide.region_11.12_spmd, body=%wide.region_9.11_spmd.sunk | while | flops 8413186 | bytes 2281725 | solution.py:55
  101.1 2.1 %fusion.69 = (f32[4]{0:T(128)S(1)}, f32[4,1024]{1,0:T(4,128)S(1)}) fusion(bf16[1024,1024]{1,0:T(8,128)(2,1)} %get-tuple-element.967, f32[4,1024]{1,0:T(4,128)S(1)} %get-tuple-element.951, f32[1024]{0:T(1024)S(1)} %get-tuple-element.966, pred[4]{0:T(512)(128)(4,1)S(1)} %compare_bitcast_fusion.13, f32[8,4,1024]{2,1,0:T(4,128)S(1)} %get-tuple-element.964, ...), kind=kOutput, calls=%fused_computation.70.clone.1 | convolution fusion | flops 8404988 | bytes 2150424 | tf_op jit(solution)/shard_map/while/body/eval_jaxpr/dot_general | solution.py:46
  103.6 2.1 %fusion.69 = (f32[4]{0:T(128)S(1)}, f32[4,1024]{1,0:T(4,128)S(1)}) fusion(bf16[1024,1024]{1,0:T(8,128)(2,1)} %get-tuple-element.967, f32[4,1024]{1,0:T(4,128)S(1)} %get-tuple-element.951, f32[1024]{0:T(1024)S(1)} %get-tuple-element.966, pred[4]{0:T(512)(128)(4,1)S(1)} %compare_bitcast_fusion.13, f32[8,4,1024]{2,1,0:T(4,128)S(1)} %get-tuple-element.964, ...), kind=kOutput, calls=%fused_computation.70.clone.1 | convolution fusion | flops 8404988 | bytes 2150424 | tf_op jit(solution)/shard_map/while/body/eval_jaxpr/dot_general | solution.py:46
  106.1 2.1 %fusion.69 = (f32[4]{0:T(128)S(1)}, f32[4,1024]{1,0:T(4,128)S(1)}) fusion(bf16[1024,1024]{1,0:T(8,128)(2,1)} %get-tuple-element.967, f32[4,1024]{1,0:T(4,128)S(1)} %get-tuple-element.951, f32[1024]{0:T(1024)S(1)} %get-tuple-element.966, pred[4]{0:T(512)(128)(4,1)S(1)} %compare_bitcast_fusion.13, f32[8,4,1024]{2,1,0:T(4,128)S(1)} %get-tuple-element.964, ...), kind=kOutput, calls=%fused_computation.70.clone.1 | convolution fusion | flops 8404988 | bytes 2150424 | tf_op jit(solution)/shard_map/while/body/eval_jaxpr/dot_general | solution.py:46
  108.6 2.1 %fusion.69 = (f32[4]{0:T(128)S(1)}, f32[4,1024]{1,0:T(4,128)S(1)}) fusion(bf16[1024,1024]{1,0:T(8,128)(2,1)} %get-tuple-element.967, f32[4,1024]{1,0:T(4,128)S(1)} %get-tuple-element.951, f32[1024]{0:T(1024)S(1)} %get-tuple-element.966, pred[4]{0:T(512)(128)(4,1)S(1)} %compare_bitcast_fusion.13, f32[8,4,1024]{2,1,0:T(4,128)S(1)} %get-tuple-element.964, ...), kind=kOutput, calls=%fused_computation.70.clone.1 | convolution fusion | flops 8404988 | bytes 2150424 | tf_op jit(solution)/shard_map/while/body/eval_jaxpr/dot_general | solution.py:46
  111.1 2.1 %fusion.69 = (f32[4]{0:T(128)S(1)}, f32[4,1024]{1,0:T(4,128)S(1)}) fusion(bf16[1024,1024]{1,0:T(8,128)(2,1)} %get-tuple-element.967, f32[4,1024]{1,0:T(4,128)S(1)} %get-tuple-element.951, f32[1024]{0:T(1024)S(1)} %get-tuple-element.966, pred[4]{0:T(512)(128)(4,1)S(1)} %compare_bitcast_fusion.13, f32[8,4,1024]{2,1,0:T(4,128)S(1)} %get-tuple-element.964, ...), kind=kOutput, calls=%fused_computation.70.clone.1 | convolution fusion | flops 8404988 | bytes 2150424 | tf_op jit(solution)/shard_map/while/body/eval_jaxpr/dot_general | solution.py:46
  113.6 2.1 %fusion.69 = (f32[4]{0:T(128)S(1)}, f32[4,1024]{1,0:T(4,128)S(1)}) fusion(bf16[1024,1024]{1,0:T(8,128)(2,1)} %get-tuple-element.967, f32[4,1024]{1,0:T(4,128)S(1)} %get-tuple-element.951, f32[1024]{0:T(1024)S(1)} %get-tuple-element.966, pred[4]{0:T(512)(128)(4,1)S(1)} %compare_bitcast_fusion.13, f32[8,4,1024]{2,1,0:T(4,128)S(1)} %get-tuple-element.964, ...), kind=kOutput, calls=%fused_computation.70.clone.1 | convolution fusion | flops 8404988 | bytes 2150424 | tf_op jit(solution)/shard_map/while/body/eval_jaxpr/dot_general | solution.py:46
  116.0 2.1 %fusion.69 = (f32[4]{0:T(128)S(1)}, f32[4,1024]{1,0:T(4,128)S(1)}) fusion(bf16[1024,1024]{1,0:T(8,128)(2,1)} %get-tuple-element.967, f32[4,1024]{1,0:T(4,128)S(1)} %get-tuple-element.951, f32[1024]{0:T(1024)S(1)} %get-tuple-element.966, pred[4]{0:T(512)(128)(4,1)S(1)} %compare_bitcast_fusion.13, f32[8,4,1024]{2,1,0:T(4,128)S(1)} %get-tuple-element.964, ...), kind=kOutput, calls=%fused_computation.70.clone.1 | convolution fusion | flops 8404988 | bytes 2150424 | tf_op jit(solution)/shard_map/while/body/eval_jaxpr/dot_general | solution.py:46
  118.5 2.1 %fusion.69 = (f32[4]{0:T(128)S(1)}, f32[4,1024]{1,0:T(4,128)S(1)}) fusion(bf16[1024,1024]{1,0:T(8,128)(2,1)} %get-tuple-element.967, f32[4,1024]{1,0:T(4,128)S(1)} %get-tuple-element.951, f32[1024]{0:T(1024)S(1)} %get-tuple-element.966, pred[4]{0:T(512)(128)(4,1)S(1)} %compare_bitcast_fusion.13, f32[8,4,1024]{2,1,0:T(4,128)S(1)} %get-tuple-element.964, ...), kind=kOutput, calls=%fused_computation.70.clone.1 | convolution fusion | flops 8404988 | bytes 2150424 | tf_op jit(solution)/shard_map/while/body/eval_jaxpr/dot_general | solution.py:46
  121.1 6.2 %while.83 = (s32[]{:T(128)}, f32[4,1024]{1,0:T(4,128)S(1)}, f32[8,4,1024]{2,0,1:T(8,128)S(1)}, s32[8,4]{1,0:T(8,128)S(1)}, f32[8,4,1024]{2,1,0:T(4,128)S(1)}, /*...) while((s32[]{:T(128)}, f32[4,1024]{1,0:T(4,128)S(1)}, ...), condition=%wide.region_20.21_spmd, body=%wide.region_18.20_spmd.sunk | while | flops 8409091 | bytes 2244781 | solution.py:68
  128.1 1.1 reshape.120
  129.2 10.6 %all_to_all.36 = bf16[2,2,8192]{2,1,0:T(2,128)(2,1)S(1)} all-to-all(bf16[2,2,8192]{2,1,0:T(2,128)(2,1)S(1)} %reshape.120), channel_id=1, replica_groups=mesh['tm'=256,'state'=2] {'state'}, dimensions={0} | all-to-all | bytes 131072 | tf_op jit(solution)/shard_map/all_to_all | solution.py:115
  139.8 1.2 reshape.121
  141.0 1.2 copy.48
  (212 shorter events, 24.3 us)
Async XLA Ops:
  7.2 10.8 %copy-start = (s32[4,16]{1,0:T(4,128)S(1)}, s32[4,16]{1,0:T(4,128)}, u32[]{:S(2)}) copy-start(s32[4,16]{1,0:T(4,128)} %param.23) | copy-start | bytes 772
  7.2 1.6 %copy-start.4 = (bf16[512]{0:T(512)(128)(2,1)S(1)}, bf16[512]{0:T(512)(128)(2,1)}, u32[]{:S(2)}) copy-start(bf16[512]{0:T(512)(128)(2,1)} %param.22) | copy-start | bytes 3076
  7.2 23.9 %all-gather.2.cloned.1.call-start = ((), (), s32[]{:S(2)}) async-start(), calls=%async_computation.2 | async-start | bytes 3170304 | tf_op jit(solution)/shard_map/all_gather | solution.py:15
  8.8 1.6 %copy-start.1 = (f32[512,512]{1,0:T(8,128)S(1)}, f32[512,512]{1,0:T(8,128)}, u32[]{:S(2)}) copy-start(f32[512,512]{1,0:T(8,128)} %param.20) | copy-start | bytes 3145732
  8.8 1.9 %copy-start.2 = (f32[512,512]{1,0:T(8,128)S(1)}, f32[512,512]{1,0:T(8,128)}, u32[]{:S(2)}) copy-start(f32[512,512]{1,0:T(8,128)} %param.19) | copy-start | bytes 3145732
  9.9 1.1 copy-start.3
  14.0 5.2 %all-to-all-start = ((f32[4,16,512]{2,0,1:T(4,128)}), f32[4,16,512]{2,0,1:T(4,128)S(1)}, u32[]{:S(2)}, u32[]{:S(2)}) async-start(f32[4,16,512]{2,0,1:T(4,128)} %copy.38), calls=%async_computation | async-start | bytes 262144 | tf_op jit(solution)/shard_map/all_to_all | solution.py:110
  58.8 9.9 %collective-permute-start = (f32[4,1024]{1,0:T(4,128)S(1)}, f32[4,1024]{1,0:T(4,128)S(1)}, u32[]{:S(2)}, u32[]{:S(2)}) collective-permute-start(f32[4,1024]{1,0:T(4,128)S(1)} %get-tuple-element.437), channel_id=1, source_target_pairs={{0,1},{1,2},{2,3},{3,4},{4,5},{5,6},{6,7},{7,8},{8,9},{9,10},{10,1... | collective-permute-start | bytes 49160 | tf_op jit(solution)/shard_map/ppermute | solution.py:26
  66.8 23.2 %collective-permute-start.2 = (f32[4,1024]{1,0:T(4,128)S(1)}, f32[4,1024]{1,0:T(4,128)S(1)}, u32[]{:S(2)}, u32[]{:S(2)}) collective-permute-start(f32[4,1024]{1,0:T(4,128)S(1)} %get-tuple-element.440), channel_id=1, source_target_pairs={{1,0},{2,1},{3,2},{4,3},{5,4},{6,5},{7,6},{8,7},{9,8},{10,9},{11,1... | collective-permute-start | bytes 49160 | tf_op jit(solution)/shard_map/ppermute | solution.py:26
  86.3 14.7 %collective-permute-start.1 = (f32[4,1024]{1,0:T(4,128)S(1)}, f32[4,1024]{1,0:T(4,128)S(1)}, u32[]{:S(2)}, u32[]{:S(2)}) collective-permute-start(f32[4,1024]{1,0:T(4,128)S(1)} %get-tuple-element.438), channel_id=1, source_target_pairs={{0,1},{1,2},{2,3},{3,4},{4,5},{5,6},{6,7},{7,8},{8,9},{9,10},{10,1... | collective-permute-start | bytes 49160 | tf_op jit(solution)/shard_map/ppermute | solution.py:26
  94.7 26.3 %collective-permute-start.3 = (f32[4,1024]{1,0:T(4,128)S(1)}, f32[4,1024]{1,0:T(4,128)S(1)}, u32[]{:S(2)}, u32[]{:S(2)}) collective-permute-start(f32[4,1024]{1,0:T(4,128)S(1)} %get-tuple-element.441), channel_id=1, source_target_pairs={{1,0},{2,1},{3,2},{4,3},{5,4},{6,5},{7,6},{8,7},{9,8},{10,9},{11,1... | collective-permute-start | bytes 49160 | tf_op jit(solution)/shard_map/ppermute | solution.py:26
Sparse Core Ops, SparseCore 0:
  10.1 20.9 all-gather.1
where the time goes:
time: 151 us; the launch traced here: 150 us
  matrix products  64.5 us (43%)
  starting transfers between devices  19.1 us (13%)
  local copies, waits for them, and re-layouts  18.4 us (12%)
  between operations  14.3 us (9%)
  waiting for transfers between devices  12.7 us (8%)
  blocking collectives  10.6 us (7%)
  other arithmetic  9.28 us (6%)
    dot_general x24, matrix products, forward_step(): jnp.dot(alpha_prev.astype(jnp.bfloat16), trans, preferred_element_type=jn...  50.3 us
    ppermute x4, starting transfers between devices, passed_along(): return lax.ppermute(block, axis, route)  15 us
    dot_general x24, matrix products, backward_step(): jnp.dot((emit_row * beta_next).astype(jnp.bfloat16), trans_back, preferre...  11.9 us
    all_gather x1, waiting for transfers between devices, in_one_piece(): lax.all_gather(both, axis, axis=dim, tiled=True)  11.7 us
    all_to_all x1, blocking collectives, per_device(): lax.all_to_all(posterior, 'state', split_axis=2, concat_axis=1, tiled=True)  10.6 us
    unnamed x15, local copies, waits for them, and re-layouts  8.69 us
    all_to_all x1, starting transfers between devices, per_device(): lax.all_to_all(scores, 'state', split_axis=1, concat_axis=2, tiled=True)  4.04 us
    transpose x1, local copies, waits for them, and re-layouts, per_device(): trans_back = trans.T  3.51 us
  transfers between devices with their start and end apart: 6, of which 2 were waited for; matrix products, arithmetic and copies ran while one was open for 34% of the time, Pallas kernels for 0%

commit v1 on v0

v1 whole, which is shorter than its diff:
```python
import jax
import jax.numpy as jnp
from jax import lax
from jax.experimental import pallas as pl
from jax.experimental.pallas import tpu as pltpu
from jax.sharding import PartitionSpec as P

MAXLEN = 16
acoustic = 0.1
VMEM = pltpu.VMEM


def split_pair(x):
    high = x.astype(jnp.bfloat16)
    return high, (x - high.astype(jnp.float32)).astype(jnp.bfloat16)


def prepare_kernel(feats, means, precs, trans, init, flags, send, keep_t, pack):
    core = lax.axis_index("state")
    half, width = means.shape
    rows = feats.shape[0]
    streams, frames = flags.shape
    init_row = init[...].astype(jnp.float32).reshape(1, half)
    for c in range(width // 128):
        at = slice(128 * c, 128 * c + 128)
        pack[c, 0:rows, :] = feats[:, at]
        pack[c, rows : rows + 8, :] = jnp.broadcast_to(init_row[:, at], (8, 128))
    flags_float = flags[...].astype(jnp.float32)
    pack[0, rows + 4 : rows + 4 + streams, 0:frames] = flags_float
    pack[0, rows + 4 : rows + 4 + streams, frames : 2 * frames] = flags_float

    prec = precs[...]
    mean = means[...]
    scaled = prec * mean
    quad_hi, quad_lo = split_pair((-0.5 * acoustic) * prec)
    lin_hi, lin_lo = split_pair(acoustic * scaled)
    send[0:half, 0:width] = quad_hi
    send[0:half, width : 2 * width] = lin_hi
    send[0:half, 2 * width : 3 * width] = quad_lo
    send[0:half, 3 * width : 4 * width] = lin_lo
    terms_hi, terms_lo = split_pair((0.5 * acoustic) * (jnp.log(prec) - scaled * mean))
    ones = jnp.ones((16, width), jnp.bfloat16)
    contract = (((1,), (1,)), ((), ()))
    offset = lax.dot_general(ones, terms_hi, contract, preferred_element_type=jnp.float32)
    offset = offset + lax.dot_general(
        ones, terms_lo, contract, preferred_element_type=jnp.float32
    )
    offset_hi, offset_lo = split_pair(offset)
    send[half : half + 16, 0:half] = offset_hi
    send[half : half + 16, half : 2 * half] = offset_lo

    straight = trans[...]
    turned_0 = trans[:, 0:half].T
    turned_1 = trans[:, half : 2 * half].T
    base = 4 * width

    @pl.when(core == 0)
    def _():
        keep_t[...] = straight
        send[0:half, base : base + half] = turned_0
        send[0:half, base + half : base + 2 * half] = turned_1

    @pl.when(core == 1)
    def _():
        send[0:half, base : base + 2 * half] = straight
        keep_t[:, 0:half] = turned_0
        keep_t[:, half : 2 * half] = turned_1


def chain_kernel(own_pack, halo_pack, own_w, own_t, other_w, out, x_tile, scores, trans, done, chain, ev, place, ordered, sems):
    core = lax.axis_index("state")
    half, states2 = own_t.shape
    states = 2 * half
    pieces = own_pack.shape[0]
    width = 128 * pieces
    rows = 2 * (own_pack.shape[1] - 8)
    frames = rows // 8
    own_rows = rows // 2
    base = 4 * width

    def assemble(index):
        copies = []
        for n, (is_own, src) in enumerate(((True, own_t), (False, other_w))):
            off = 0 if is_own else base
            at = index if is_own else 1 - index
            for piece in range(2):
                part = src.at[0:half, off + piece * half : off + (piece + 1) * half]
                if index == 0:
                    target = trans.at[at * half : (at + 1) * half, piece * half : (piece + 1) * half]
                else:
                    target = trans.at[piece * half : (piece + 1) * half, at * half : (at + 1) * half]
                copies.append(pltpu.make_async_copy(part, target, sems.at[2 * n + piece]))
        return copies

    @pl.when(core == 0)
    def _():
        for copy in assemble(0):
            copy.start()

    @pl.when(core == 1)
    def _():
        for copy in assemble(1):
            copy.start()

    for j in range(frames):
        at = jnp.where(core == 0, j, frames - 1 - j)
        for c in range(pieces):
            cols = slice(128 * c, 128 * c + 128)
            x_tile[8 * j : 8 * j + 4, cols] = halo_pack[c, pl.ds(at, 4, stride=frames), :]
            x_tile[8 * j + 4 : 8 * j + 8, cols] = own_pack[c, pl.ds(at, 4, stride=frames), :]

    lane = lax.broadcasted_iota(jnp.int32, (4, 128), 1)
    flag4 = jnp.where(
        lane < frames,
        halo_pack[0, own_rows + 4 : own_rows + 8, :],
        own_pack[0, own_rows + 4 : own_rows + 8, :],
    )
    flag4 = jnp.where(lane < 2 * frames, flag4, 0.0)
    flag8 = jnp.concatenate([flag4, flag4], axis=0)
    lane8 = lax.broadcasted_iota(jnp.int32, (8, 128), 1)
    part = jnp.where(lane8 < frames, 0, frames)
    inside = lane8 - part
    when = part + jnp.where(core == 0, inside, frames - 1 - inside) + core
    sub8 = lax.broadcasted_iota(jnp.int32, (8, 128), 0)
    for j in range(frames):
        mine = jnp.where(sub8 < 4, j, frames + j)
        starts = jnp.where((flag8 > 0.5) & (when <= mine), when, -1000)
        last = jnp.max(starts.astype(jnp.float32), axis=1, keepdims=True)
        place[8 * j : 8 * j + 8, :] = mine.astype(jnp.float32) - last

    x = x_tile[...]
    x_hi, x_lo = split_pair(x)
    q_hi, q_lo = split_pair(x * x)
    both = jnp.concatenate(
        [jnp.concatenate([q_hi, x_hi], axis=1), jnp.concatenate([q_lo, x_lo], axis=1)], axis=0
    )
    contract = (((1,), (1,)), ((), ()))

    def half_scores(w):
        main = lax.dot_general(
            both, w[0:half, 0 : 2 * width], contract, preferred_element_type=jnp.float32
        )
        rest = lax.dot_general(
            both[0:rows],
            w[0:half, 2 * width : 4 * width],
            contract,
            preferred_element_type=jnp.float32,
        )
        offset = w[half : half + 1, 0:half].astype(jnp.float32) + w[
            half : half + 1, half : 2 * half
        ].astype(jnp.float32)
        return main[0:rows] + (main[rows : 2 * rows] + rest) + offset

    scores[:, pl.ds(pl.multiple_of(core * half, half), half)] = half_scores(own_w)
    scores[:, pl.ds(pl.multiple_of((1 - core) * half, half), half)] = half_scores(other_w)
    s = scores[...]
    emission = jnp.exp(s - jnp.max(s, axis=1, keepdims=True))
    scores[...] = emission

    line = slice(own_rows, own_rows + 1)
    init_parts = [own_pack[c, line, :] for c in range(pieces)]
    init_parts += [halo_pack[c, line, :] for c in range(pieces)]
    init_row = jnp.where(core == 0, jnp.concatenate(init_parts, axis=1), 1.0)
    prior = init_row / jnp.sum(init_row, axis=1, keepdims=True)

    def finish(k, predicted):
        weighted = scores[...] * predicted
        norm = jnp.sum(weighted, axis=1, keepdims=True)
        alpha = weighted * (1.0 / norm)
        mask = place[...] == k.astype(jnp.float32)
        result = jnp.where(core == 0, alpha, predicted)
        for c in range(states // 128):
            at = slice(128 * c, 128 * c + 128)
            done[:, at] = jnp.where(mask, result[:, at], done[:, at])
        ev[...] = jnp.where(mask, jnp.log(norm), ev[...])
        turned = jnp.concatenate(
            [alpha[rows - 4 : rows], alpha[rows - 8 : rows - 4], alpha[0 : rows - 8]], axis=0
        )
        chain[...] = turned.astype(jnp.bfloat16)

    done[...] = jnp.zeros_like(done)
    ev[...] = jnp.zeros_like(ev)
    finish(jnp.int32(0), jnp.broadcast_to(prior, (rows, states)))

    @pl.when(core == 0)
    def _():
        for copy in assemble(0):
            copy.wait()

    @pl.when(core == 1)
    def _():
        for copy in assemble(1):
            copy.wait()

    def step(k, carry):
        finish(k, jnp.dot(chain[...], trans[...], preferred_element_type=jnp.float32))
        return carry

    lax.fori_loop(1, MAXLEN, step, 0)

    for j in range(frames):
        at = jnp.where(core == 0, j, frames - 1 - j)
        for c in range(states // 128):
            cols = slice(128 * c, 128 * c + 128)
            ordered[c, pl.ds(at, 4, stride=frames), :] = done[8 * j + 4 : 8 * j + 8, cols]
        ordered[states // 128, pl.ds(at, 4, stride=frames), :] = ev[8 * j + 4 : 8 * j + 8, :]
    for c in range(states // 128):
        out[:, 128 * c : 128 * c + 128] = ordered[c].astype(jnp.bfloat16)
    ev_hi, ev_lo = split_pair(ordered[states // 128])
    out[:, states : states + 128] = ev_hi
    out[:, states + 128 : states + 256] = ev_lo


def combine_kernel(own, other, posterior, evidence):
    core = lax.axis_index("state")
    streams, frames, half = posterior.shape
    states = 2 * half
    product = own[:, 0:states].astype(jnp.float32) * other[:, 0:states].astype(jnp.float32)
    inverse = 1.0 / jnp.sum(product, axis=1, keepdims=True)
    mine = jnp.where(core == 0, product[:, 0:half], product[:, half:states])
    posterior[...] = (mine * inverse).astype(jnp.bfloat16).reshape(streams, frames, half)

    def pair(ref):
        return ref[:, states : states + 128].astype(jnp.float32) + ref[
            :, states + 128 : states + 256
        ].astype(jnp.float32)

    logs = jnp.where(core == 0, pair(own), pair(other))
    shape = (streams * frames, 128)
    row = lax.broadcasted_iota(jnp.int32, shape, 0)
    lane = lax.broadcasted_iota(jnp.int32, shape, 1)
    kept = jnp.where(row % frames == lane + core * (frames // 2), logs, 0.0)
    for b in range(streams):
        line = jnp.sum(kept[b * frames : (b + 1) * frames], axis=0, keepdims=True)
        evidence[b : b + 1, :] = line[:, 0 : frames // 2]


def whole(count):
    return [pl.BlockSpec(memory_space=VMEM)] * count


def per_device(features, gauss_means, precisions, transitions, initial, reset_flags):
    streams, frames, width = features.shape
    half = gauss_means.shape[0]
    states = transitions.shape[1]
    rows = streams * frames
    blocks = lax.axis_size("tm")
    devices = 2 * blocks
    bf16, f32 = jnp.bfloat16, jnp.float32

    send, keep_t, pack = pl.pallas_call(
        prepare_kernel,
        out_shape=(
            jax.ShapeDtypeStruct((half + 16, 4 * width + states), bf16),
            jax.ShapeDtypeStruct((half, states), bf16),
            jax.ShapeDtypeStruct((width // 128, rows + 8, 128), f32),
        ),
        in_specs=whole(6),
        out_specs=tuple(whole(3)),
        name="prepare",
    )(features.reshape(rows, width), gauss_means, precisions, transitions, initial, reset_flags)

    neighbours = []
    for i in range(blocks):
        before = (2 * i - 1) % devices
        neighbours += [(before, 2 * i), (2 * i, before)]
    halo = lax.ppermute(pack, ("tm", "state"), neighbours)
    other = lax.ppermute(send, "state", [(0, 1), (1, 0)])

    out = pl.pallas_call(
        chain_kernel,
        out_shape=jax.ShapeDtypeStruct((rows, states + 256), bf16),
        in_specs=whole(5),
        out_specs=whole(1)[0],
        scratch_shapes=[
            VMEM((2 * rows, width), f32),
            VMEM((2 * rows, states), f32),
            VMEM((states, states), bf16),
            VMEM((2 * rows, states), f32),
            VMEM((2 * rows, states), bf16),
            VMEM((2 * rows, 128), f32),
            VMEM((2 * rows, 128), f32),
            VMEM((states // 128 + 1, rows, 128), f32),
            pltpu.SemaphoreType.DMA((4,)),
        ],
        name="chain",
    )(pack, halo, send, keep_t, other)

    out_other = lax.ppermute(out, "state", [(0, 1), (1, 0)])
    return pl.pallas_call(
        combine_kernel,
        out_shape=(
            jax.ShapeDtypeStruct((streams, frames, half), bf16),
            jax.ShapeDtypeStruct((streams, frames // 2), f32),
        ),
        in_specs=whole(2),
        out_specs=tuple(whole(2)),
        name="combine",
    )(out, out_other)


def solution(mesh):
    return jax.shard_map(
        per_device,
        mesh=mesh,
        in_specs=(
            P(None, "tm", None),
            P("state", None),
            P("state", None),
            P("state", None),
            P("state"),
            P(None, "tm"),
        ),
        out_specs=(P(None, "tm", "state"), P(None, ("tm", "state"))),
        check_vma=False,
    )
```

time: 151 us -> 50.9 us (0.34)
  the two profiles are of different devices: /device:TPU:257 before, /device:TPU:1 now
where the time goes in v1:
time: 50.9 us; the launch traced here: 50.7 us
  Pallas kernels  21.9 us (43%)
  starting transfers between devices  19.7 us (39%)
  waiting for transfers between devices  5.96 us (12%)
  local copies, waits for them, and re-layouts  2.43 us (5%)
  between operations  0.67 us (1%)
    pallas_call x1, Pallas kernels, per_device(): pl.pallas_call(chain_kernel, out_shape=jax.ShapeDtypeStruct((rows, states...  15.1 us
    ppermute x1, starting transfers between devices, per_device(): out_other = lax.ppermute(out, 'state', [(0, 1), (1, 0)])  9.1 us
    ppermute x1, starting transfers between devices, per_device(): other = lax.ppermute(send, 'state', [(0, 1), (1, 0)])  8.73 us
    pallas_call x1, Pallas kernels, per_device(): pl.pallas_call(prepare_kernel, out_shape=(jax.ShapeDtypeStruct((half + 16...  5.07 us
    ppermute x1, waiting for transfers between devices, per_device(): halo = lax.ppermute(pack, ('tm', 'state'), neighbours)  4.74 us
    unnamed x6, local copies, waits for them, and re-layouts  2.43 us
    ppermute x1, starting transfers between devices, per_device(): halo = lax.ppermute(pack, ('tm', 'state'), neighbours)  1.92 us
    pallas_call x1, Pallas kernels, per_device(): pl.pallas_call(combine_kernel, out_shape=(jax.ShapeDtypeStruct((streams,...  1.75 us
  transfers between devices with their start and end apart: 3, of which 2 were waited for; matrix products, arithmetic and copies ran while one was open for 0% of the time, Pallas kernels for 0%

profile of v1, /device:TPU:1, one launch (start us, length us, event | category | flops | bytes accessed | tf_op | source)
XLA Modules:
  0.0 50.7 jit_solution(5613662566406600196)
XLA Ops:
  0.6 5.1 %prepare.1 = (bf16[528,3072]{1,0:T(8,128)(2,1)}, bf16[512,1024]{1,0:T(8,128)(2,1)}, f32[4,72,128]{2,1,0:T(8,128)}) custom-call(f32[64,512]{1,0:T(8,128)} %bitcast.1, f32[512,512]{1,0:T(8,128)} %means.1, f32[512,512]{1,0:T(8,128)} %precs.1, bf16[512,1024]{1,0:T(8,128)(2,1)} %trans.1, bf16[512]{0:T(512)(128)(2,1)} %init.1, s32[4,16]{1,0:T(4,128)} %flags.1), custom_call_target="tpu_custom_call" | custom-call | tf_op jit(solution)/shard_map/prepare/pallas_call | solution.py:251
  5.7 8.7 %collective-permute-start.1 = (bf16[528,3072]{1,0:T(8,128)(2,1)}, bf16[528,3072]{1,0:T(8,128)(2,1)S(1)}, u32[]{:S(2)}, u32[]{:S(2)}) collective-permute-start(bf16[528,3072]{1,0:T(8,128)(2,1)} %get-tuple-element.6.own_w), channel_id=1, source_target_pairs={{0,1},{1,0},{2,3},{3,2},{4,5},{5,4},{6,7},{7,6},{8,9},{9,8},{10,11... | collective-permute-start | bytes 9732104 | tf_op jit(solution)/shard_map/ppermute | solution.py:268
  14.4 1.9 %collective-permute-start = (f32[4,72,128]{2,1,0:T(8,128)}, f32[4,72,128]{2,1,0:T(8,128)S(1)}, u32[]{:S(2)}, u32[]{:S(2)}) collective-permute-start(f32[4,72,128]{2,1,0:T(8,128)} %get-tuple-element.5.own_pack), channel_id=1, source_target_pairs={{511,0},{0,511},{1,2},{2,1},{3,4},{4,3},{5,6},{6,5},{7,8},{8,7},{9... | collective-permute-start | bytes 442376 | tf_op jit(solution)/shard_map/ppermute | solution.py:267
  16.4 4.7 %collective-permute-done.halo_pack = f32[4,72,128]{2,1,0:T(8,128)S(1)} collective-permute-done((f32[4,72,128]{2,1,0:T(8,128)}, f32[4,72,128]{2,1,0:T(8,128)S(1)}, u32[]{:S(2)}, u32[]{:S(2)}) %collective-permute-start) | collective-permute-done | bytes 147488 | tf_op jit(solution)/shard_map/ppermute | solution.py:267
  21.1 0.0 copy-start.2
  21.1 0.0 collective-permute-done.1.other_w
  21.1 0.0 copy-start
  21.1 0.7 %copy-done.2 = f32[4,72,128]{2,1,0:T(8,128)} copy-done((f32[4,72,128]{2,1,0:T(8,128)}, f32[4,72,128]{2,1,0:T(8,128)S(1)}, u32[]{:S(2)}) %copy-start.2) | copy-done | bytes 147480
  21.8 1.1 %copy-done = bf16[528,3072]{1,0:T(8,128)(2,1)} copy-done((bf16[528,3072]{1,0:T(8,128)(2,1)}, bf16[528,3072]{1,0:T(8,128)(2,1)S(1)}, u32[]{:S(2)}) %copy-start) | copy-done | bytes 3244056
  22.9 15.1 %chain.1.own = bf16[64,1280]{1,0:T(8,128)(2,1)} custom-call(f32[4,72,128]{2,1,0:T(8,128)} %get-tuple-element.5.own_pack, f32[4,72,128]{2,1,0:T(8,128)} %copy-done.2, bf16[528,3072]{1,0:T(8,128)(2,1)} %get-tuple-element.6.own_w, bf16[512,1024]{1,0:T(8,128)(2,1)} %get-tuple-element.7.own_t, bf16[528,3072]{1,0:T(8,128)(2,1)} %copy-done), custom_call_target="tpu_custom_call" | custom-call | tf_op jit(solution)/shard_map/chain/pallas_call | solution.py:270
  38.0 9.1 %collective-permute-start.2 = (bf16[64,1280]{1,0:T(8,128)(2,1)}, bf16[64,1280]{1,0:T(8,128)(2,1)S(1)}, u32[]{:S(2)}, u32[]{:S(2)}) collective-permute-start(bf16[64,1280]{1,0:T(8,128)(2,1)} %chain.1.own), channel_id=1, source_target_pairs={{0,1},{1,0},{2,3},{3,2},{4,5},{5,4},{6,7},{7,6},{8,9},{9,8},{10,11... | collective-permute-start | bytes 491528 | tf_op jit(solution)/shard_map/ppermute | solution.py:289
  47.1 1.2 %collective-permute-done.2.other = bf16[64,1280]{1,0:T(8,128)(2,1)S(1)} collective-permute-done((bf16[64,1280]{1,0:T(8,128)(2,1)}, bf16[64,1280]{1,0:T(8,128)(2,1)S(1)}, u32[]{:S(2)}, u32[]{:S(2)}) %collective-permute-start.2) | collective-permute-done | bytes 163872 | tf_op jit(solution)/shard_map/ppermute | solution.py:289
  48.3 0.0 copy-start.1
  48.3 0.7 %copy-done.1 = bf16[64,1280]{1,0:T(8,128)(2,1)} copy-done((bf16[64,1280]{1,0:T(8,128)(2,1)}, bf16[64,1280]{1,0:T(8,128)(2,1)S(1)}, u32[]{:S(2)}) %copy-start.1) | copy-done | bytes 163864
  49.0 1.7 %combine.1 = (bf16[4,16,512]{2,1,0:T(8,128)(2,1)}, f32[4,8]{1,0:T(4,128)}) custom-call(bf16[64,1280]{1,0:T(8,128)(2,1)} %chain.1.own, bf16[64,1280]{1,0:T(8,128)(2,1)} %copy-done.1), custom_call_target="tpu_custom_call" | custom-call | tf_op jit(solution)/shard_map/combine/pallas_call | solution.py:290
Async XLA Ops:
  5.7 15.4 %collective-permute-start.1 = (bf16[528,3072]{1,0:T(8,128)(2,1)}, bf16[528,3072]{1,0:T(8,128)(2,1)S(1)}, u32[]{:S(2)}, u32[]{:S(2)}) collective-permute-start(bf16[528,3072]{1,0:T(8,128)(2,1)} %get-tuple-element.6.own_w), channel_id=1, source_target_pairs={{0,1},{1,0},{2,3},{3,2},{4,5},{5,4},{6,7},{7,6},{8,9},{9,8},{10,11... | collective-permute-start | bytes 9732104 | tf_op jit(solution)/shard_map/ppermute | solution.py:268
  14.4 6.7 %collective-permute-start = (f32[4,72,128]{2,1,0:T(8,128)}, f32[4,72,128]{2,1,0:T(8,128)S(1)}, u32[]{:S(2)}, u32[]{:S(2)}) collective-permute-start(f32[4,72,128]{2,1,0:T(8,128)} %get-tuple-element.5.own_pack), channel_id=1, source_target_pairs={{511,0},{0,511},{1,2},{2,1},{3,4},{4,3},{5,6},{6,5},{7,8},{8,7},{9... | collective-permute-start | bytes 442376 | tf_op jit(solution)/shard_map/ppermute | solution.py:267
  21.1 0.7 %copy-start.2 = (f32[4,72,128]{2,1,0:T(8,128)}, f32[4,72,128]{2,1,0:T(8,128)S(1)}, u32[]{:S(2)}) copy-start(f32[4,72,128]{2,1,0:T(8,128)S(1)} %collective-permute-done.halo_pack) | copy-start | bytes 442372
  21.1 1.8 %copy-start = (bf16[528,3072]{1,0:T(8,128)(2,1)}, bf16[528,3072]{1,0:T(8,128)(2,1)S(1)}, u32[]{:S(2)}) copy-start(bf16[528,3072]{1,0:T(8,128)(2,1)S(1)} %collective-permute-done.1.other_w) | copy-start | bytes 9732100
  38.0 10.3 %collective-permute-start.2 = (bf16[64,1280]{1,0:T(8,128)(2,1)}, bf16[64,1280]{1,0:T(8,128)(2,1)S(1)}, u32[]{:S(2)}, u32[]{:S(2)}) collective-permute-start(bf16[64,1280]{1,0:T(8,128)(2,1)} %chain.1.own), channel_id=1, source_target_pairs={{0,1},{1,0},{2,3},{3,2},{4,5},{5,4},{6,7},{7,6},{8,9},{9,8},{10,11... | collective-permute-start | bytes 491528 | tf_op jit(solution)/shard_map/ppermute | solution.py:289
  48.3 0.7 %copy-start.1 = (bf16[64,1280]{1,0:T(8,128)(2,1)}, bf16[64,1280]{1,0:T(8,128)(2,1)S(1)}, u32[]{:S(2)}) copy-start(bf16[64,1280]{1,0:T(8,128)(2,1)S(1)} %collective-permute-done.2.other) | copy-start | bytes 491524

commit v2 on v0

v2 whole, which is shorter than its diff:
```python
import jax
import jax.numpy as jnp
from jax import lax
from jax.experimental import pallas as pl
from jax.experimental.pallas import tpu as pltpu
from jax.sharding import PartitionSpec as P


MAXLEN = 16
acoustic = 0.1
VMEM = pltpu.VMEM
MIB = 1 << 20
CHUNKS = 4
UNROLL = 3
SCALE = 2.0**108
TRANSPOSED = (((1,), (1,)), ((), ()))
bf16, f32 = jnp.bfloat16, jnp.float32


def split_pair(x):
    high = x.astype(bf16)
    return high, (x - high.astype(f32)).astype(bf16)


def weights_kernel(
    feats, means, precs, flags, init, pack, w_send, prec_in, mean_in, flag_in, init_in, sems
):
    half, width = means.shape
    rows = feats.shape[0]
    streams, frames = flags.shape
    step = half // CHUNKS
    pieces = width // 128
    copies = []
    for n in range(CHUNKS):
        at = slice(n * step, (n + 1) * step)
        copies.append(pltpu.make_async_copy(precs.at[at], prec_in.at[at], sems.at[2 * n]))
        copies.append(pltpu.make_async_copy(means.at[at], mean_in.at[at], sems.at[2 * n + 1]))
    for c in range(pieces):
        part = feats.at[:, 128 * c : 128 * c + 128]
        copies.append(
            pltpu.make_async_copy(part, pack.at[c, 0:rows], sems.at[2 * CHUNKS + c])
        )
    copies.append(pltpu.make_async_copy(flags, flag_in, sems.at[2 * CHUNKS + pieces]))
    copies.append(pltpu.make_async_copy(init, init_in, sems.at[2 * CHUNKS + pieces + 1]))
    for copy in copies:
        copy.start()

    ones = jnp.ones((16, width), bf16)
    for n in range(CHUNKS):
        copies[2 * n].wait()
        copies[2 * n + 1].wait()
        r = n * step
        at = slice(r, r + step)
        prec = prec_in[at, :]
        mean = mean_in[at, :]
        scaled = prec * mean
        quad_hi, quad_lo = split_pair((-0.5 * acoustic) * prec)
        lin_hi, lin_lo = split_pair(acoustic * scaled)
        w_send[at, 0:width] = quad_hi
        w_send[at, width : 2 * width] = lin_hi
        w_send[at, 2 * width : 3 * width] = quad_lo
        w_send[at, 3 * width : 4 * width] = lin_lo
        terms_hi, terms_lo = split_pair((0.5 * acoustic) * (jnp.log(prec) - scaled * mean))
        offset = lax.dot_general(ones, terms_hi, TRANSPOSED, preferred_element_type=f32)
        offset = offset + lax.dot_general(ones, terms_lo, TRANSPOSED, preferred_element_type=f32)
        offset_hi, offset_lo = split_pair(offset)
        w_send[half : half + 16, r : r + step] = offset_hi
        w_send[half : half + 16, half + r : half + r + step] = offset_lo
    for copy in copies[2 * CHUNKS :]:
        copy.wait()
    w_send[half : half + 16, 2 * half : 3 * half] = jnp.broadcast_to(
        init_in[...].astype(f32).reshape(1, half), (16, half)
    ).astype(bf16)
    w_send[half : half + 16, 3 * half : 4 * half] = jnp.zeros((16, half), bf16)
    flags_float = flag_in[...].astype(f32)
    pack[0, rows : rows + 8, :] = jnp.zeros((8, 128), f32)
    pack[0, rows + 4 : rows + 4 + streams, 0:frames] = flags_float
    pack[0, rows + 4 : rows + 4 + streams, frames : 2 * frames] = flags_float


def turn_kernel(trans, t_send, t_keep):
    core = lax.axis_index("state")
    half = trans.shape[0]
    turned_0 = trans[:, 0:half].T
    turned_1 = trans[:, half : 2 * half].T

    @pl.when(core == 0)
    def _():
        t_keep[...] = trans[...]
        t_send[:, 0:half] = turned_1
        t_send[:, half : 2 * half] = turned_0

    @pl.when(core == 1)
    def _():
        t_send[...] = trans[...]
        t_keep[:, 0:half] = turned_1
        t_keep[:, half : 2 * half] = turned_0


def half_scores(both, w):
    width = w.shape[1] // 4
    half = w.shape[0] - 16
    rows = both.shape[0] // 2
    main = lax.dot_general(
        both[...], w[0:half, 0 : 2 * width], TRANSPOSED, preferred_element_type=f32
    )
    rest = lax.dot_general(
        both[0:rows, :],
        w[0:half, 2 * width : 4 * width],
        TRANSPOSED,
        preferred_element_type=f32,
    )
    extra = w[half : half + 1, 0 : 2 * half].astype(f32)
    return main[0:rows] + (main[rows : 2 * rows] + rest) + (extra[:, 0:half] + extra[:, half:])


def scores_kernel(own_pack, halo_pack, own_w, both, scores, place):
    core = lax.axis_index("state")
    is_last = lax.axis_index("tm") == lax.axis_size("tm") - 1
    pieces = own_pack.shape[0]
    width = 128 * pieces
    own_rows = own_pack.shape[1] - 8
    rows = 2 * own_rows
    frames = rows // 8

    lane = lax.broadcasted_iota(jnp.int32, (4, 128), 1)
    end_reset = jnp.where((core == 1) & is_last, 1.0, 0.0)
    flag4 = jnp.where(
        lane < frames,
        jnp.maximum(halo_pack[0, own_rows + 4 : own_rows + 8, :], end_reset),
        own_pack[0, own_rows + 4 : own_rows + 8, :],
    )
    flag4 = jnp.where(lane < 2 * frames, flag4, 0.0)
    flag8 = jnp.concatenate([flag4, flag4], axis=0)
    lane8 = lax.broadcasted_iota(jnp.int32, (8, 128), 1)
    part = jnp.where(lane8 < frames, 0, frames)
    inside = lane8 - part
    when = part + jnp.where(core == 0, inside, frames - 1 - inside) + core
    sub8 = lax.broadcasted_iota(jnp.int32, (8, 128), 0)
    for j in range(frames):
        mine = jnp.where(sub8 < 4, j, frames + j)
        starts = jnp.where((flag8 > 0.5) & (when <= mine), when, -1000)
        last = jnp.max(starts.astype(f32), axis=1, keepdims=True)
        place[8 * j : 8 * j + 8, :] = mine.astype(f32) - last

    for c in range(pieces):
        tiles = []
        for j in range(frames):
            at = jnp.where(core == 0, j, frames - 1 - j)
            tiles.append(halo_pack[c, pl.ds(at, 4, stride=frames), :])
            tiles.append(own_pack[c, pl.ds(at, 4, stride=frames), :])
        x = jnp.concatenate(tiles, axis=0)
        x_hi, x_lo = split_pair(x)
        q_hi, q_lo = split_pair(x * x)
        cols = slice(128 * c, 128 * c + 128)
        past = slice(width + 128 * c, width + 128 * c + 128)
        both[0:rows, cols] = q_hi
        both[0:rows, past] = x_hi
        both[rows : 2 * rows, cols] = q_lo
        both[rows : 2 * rows, past] = x_lo
    scores[...] = half_scores(both, own_w)


def emission_kernel(both, own_scores, other_w, emission):
    half = own_scores.shape[1]
    other_scores = half_scores(both, other_w)
    mine = own_scores[...]
    top = jnp.maximum(
        jnp.max(mine, axis=1, keepdims=True), jnp.max(other_scores, axis=1, keepdims=True)
    )
    emission[:, 0:half] = jnp.exp(mine - top)
    emission[:, half : 2 * half] = jnp.exp(other_scores - top)


def chain_kernel(
    emission, place, own_w, other_w, own_t, other_t, out, chain, done, part, gain, sums, gains, ordered
):
    core = lax.axis_index("state")
    half, states = own_t.shape
    rows = place.shape[0]
    frames = rows // 8
    shape = (rows, 128)

    def advance(x):
        last = x[rows - 8 : rows]
        return jnp.concatenate([last[4:8], last[0:4], x[0 : rows - 8]], axis=0)

    def settle(k):
        total = jnp.broadcast_to(jnp.sum(part[...], axis=1, keepdims=True) * gain[...], shape)
        sums[...] = jnp.where(place[...] == k - 1.0, total, sums[...])
        return total

    def spread(k, predicted, scale, index):
        mask = place[...] == k
        sum_tile = None
        for c in range(states // 128):
            at = slice(128 * c, 128 * c + 128)
            ahead = predicted[:, at]
            weighted = ahead * emission[:, at]
            sum_tile = weighted if sum_tile is None else sum_tile + weighted
            result = weighted if index == 0 else ahead
            done[:, at] = jnp.where(mask, result, done[:, at])
            chain[:, at] = advance(weighted * scale).astype(bf16)
        part[...] = sum_tile

    def run(index):
        if index == 0:
            line = slice(half, half + 1)
            first = jnp.concatenate(
                [w[line, 2 * half : 3 * half].astype(f32) for w in (own_w, other_w)], axis=1
            )
            first = first / jnp.sum(first, axis=1, keepdims=True)
        else:
            first = jnp.full((1, states), 1.0 / states, f32)
        gain[...] = jnp.full(shape, SCALE, f32)
        gains[...] = jnp.full(shape, SCALE, f32)
        sums[...] = jnp.full(shape, SCALE, f32)
        done[...] = jnp.zeros_like(done)
        spread(0.0, jnp.broadcast_to(first, (rows, states)), SCALE, index)

        def step(k, carry):
            k = k.astype(f32)
            total = settle(k)
            scale = SCALE / advance(total)
            gain[...] = scale
            gains[...] = jnp.where(place[...] == k, scale, gains[...])
            mine, theirs = chain[:, 0:half], chain[:, half:states]
            if index == 0:
                blocks = (own_t[:, 0:half], other_t[:, 0:half], own_t[:, half:], other_t[:, half:])
            else:
                blocks = (own_t[:, 0:half], own_t[:, half:], other_t[:, 0:half], other_t[:, half:])
            predicted = jnp.concatenate(
                [
                    jnp.dot(mine, blocks[2 * n], preferred_element_type=f32)
                    + jnp.dot(theirs, blocks[2 * n + 1], preferred_element_type=f32)
                    for n in range(2)
                ],
                axis=1,
            )
            spread(k, predicted, scale, index)
            return carry

        lax.fori_loop(1, MAXLEN, step, 0, unroll=UNROLL)
        settle(float(MAXLEN))
        norm = sums[...]
        scale = gains[...] / norm if index == 0 else gains[...] * (1.0 / SCALE)
        logs = jnp.log(norm * (1.0 / SCALE))
        last = states // 128
        for j in range(frames):
            at = j if index == 0 else frames - 1 - j
            own = slice(8 * j + 4, 8 * j + 8)
            for c in range(last):
                cols = slice(128 * c, 128 * c + 128)
                ordered[c, pl.ds(at, 4, stride=frames), :] = done[own, cols] * scale[own]
            ordered[last, pl.ds(at, 4, stride=frames), :] = logs[own]
        for c in range(last):
            out[:, 128 * c : 128 * c + 128] = ordered[c].astype(bf16)
        logs_hi, logs_lo = split_pair(ordered[last])
        out[:, states : states + 128] = logs_hi
        out[:, states + 128 : states + 256] = logs_lo

    for index in range(2):

        @pl.when(core == index)
        def _():
            run(index)


def combine_kernel(own, other, posterior, evidence):
    core = lax.axis_index("state")
    streams, frames, half = posterior.shape
    states = 2 * half
    mine = own[:, 0:half].astype(f32) * other[:, half:states].astype(f32)
    theirs = own[:, half:states].astype(f32) * other[:, 0:half].astype(f32)
    inverse = 1.0 / jnp.sum(mine + theirs, axis=1, keepdims=True)
    posterior[...] = (mine * inverse).astype(bf16).reshape(streams, frames, half)

    def pair(ref):
        return ref[:, states : states + 128].astype(f32) + ref[
            :, states + 128 : states + 256
        ].astype(f32)

    logs = jnp.where(core == 0, pair(own), pair(other))
    shape = (streams * frames, 128)
    row = lax.broadcasted_iota(jnp.int32, shape, 0)
    lane = lax.broadcasted_iota(jnp.int32, shape, 1)
    kept = jnp.where(row % frames == lane + core * (frames // 2), logs, 0.0)
    for b in range(streams):
        line = jnp.sum(kept[b * frames : (b + 1) * frames], axis=0, keepdims=True)
        evidence[b : b + 1, :] = line[:, 0 : frames // 2]


def kernel(body, outs, scratch, vmem, cost, *args, hbm=()):
    in_vmem = pl.BlockSpec(memory_space=VMEM)
    in_hbm = pl.BlockSpec(memory_space=pltpu.HBM)
    args = [
        pltpu.with_memory_space_constraint(a, pltpu.HBM) if n in hbm else a
        for n, a in enumerate(args)
    ]
    return pl.pallas_call(
        body,
        out_shape=[jax.ShapeDtypeStruct(*o) for o in outs],
        in_specs=[in_hbm if n in hbm else in_vmem for n in range(len(args))],
        out_specs=[in_vmem] * len(outs),
        scratch_shapes=scratch,
        compiler_params=pltpu.CompilerParams(vmem_limit_bytes=vmem * MIB),
        cost_estimate=pl.CostEstimate(flops=cost, bytes_accessed=1 * MIB, transcendentals=0),
    )(*args)


def per_device(features, gauss_means, precisions, transitions, initial, reset_flags):
    streams, frames, width = features.shape
    half = gauss_means.shape[0]
    states = transitions.shape[1]
    rows = streams * frames
    blocks = lax.axis_size("tm")
    partner = [(0, 1), (1, 0)]

    pack, w_send = kernel(
        weights_kernel,
        [((width // 128, rows + 8, 128), f32), ((half + 16, 4 * width), bf16)],
        [
            VMEM((half, width), f32),
            VMEM((half, width), f32),
            VMEM((streams, frames), jnp.int32),
            VMEM((half,), bf16),
            pltpu.SemaphoreType.DMA((2 * CHUNKS + width // 128 + 2,)),
        ],
        16, 10**9,
        features.reshape(rows, width), gauss_means, precisions, reset_flags, initial,
        hbm=range(5),
    )
    pairs = [(2 * i - 1, 2 * i) for i in range(1, blocks)]
    halo = lax.ppermute(pack, ("tm", "state"), pairs + [(b, a) for a, b in pairs])
    other_w = lax.ppermute(w_send, "state", partner)
    t_send, t_keep = kernel(
        turn_kernel,
        [((half, states), bf16), ((half, states), bf16)],
        [], 16, 10**9,
        transitions,
    )
    other_t = lax.ppermute(t_send, "state", partner)
    both, scores, place = kernel(
        scores_kernel,
        [((4 * rows, 2 * width), bf16), ((2 * rows, half), f32), ((2 * rows, 128), f32)],
        [], 16, 10**9,
        pack, halo, w_send,
    )
    (emission,) = kernel(
        emission_kernel, [((2 * rows, states), f32)], [], 16, 10**9,
        both, scores, other_w,
    )
    wide, narrow = VMEM((2 * rows, states), f32), VMEM((2 * rows, 128), f32)
    (out,) = kernel(
        chain_kernel,
        [((rows, states + 256), bf16)],
        [
            VMEM((2 * rows, states), bf16),
            wide, narrow, narrow, narrow, narrow,
            VMEM((states // 128 + 1, rows, 128), f32),
        ],
        24, 10**10,
        emission, place, w_send, other_w, t_keep, other_t,
    )
    out_other = lax.ppermute(out, "state", partner)
    posterior, evidence = kernel(
        combine_kernel,
        [((streams, frames, half), bf16), ((streams, frames // 2), f32)],
        [], 8, 10**6,
        out, out_other,
    )
    return posterior, evidence


def solution(mesh):
    return jax.shard_map(
        per_device,
        mesh=mesh,
        in_specs=(
            P(None, "tm", None),
            P("state", None),
            P("state", None),
            P("state", None),
            P("state"),
            P(None, "tm"),
        ),
        out_specs=(P(None, "tm", "state"), P(None, ("tm", "state"))),
        check_vma=False,
    )
```

time: 151 us -> 34.4 us (0.23)
  the two profiles are of different devices: /device:TPU:257 before, /device:TPU:1 now
where the time goes in v2:
time: 34.4 us; the launch traced here: 34.2 us
  starting transfers between devices  14.5 us (42%)
  Pallas kernels  13.1 us (38%)
  waiting for transfers between devices  5.9 us (17%)
  between operations  0.73 us (2%)
    pallas_call x6, Pallas kernels, kernel(): pl.pallas_call(body, out_shape=[jax.ShapeDtypeStruct(*o) for o in outs],...  13.1 us
    ppermute x1, starting transfers between devices, per_device(): other_w = lax.ppermute(w_send, 'state', partner)  8.75 us
    ppermute x1, waiting for transfers between devices, per_device(): lax.ppermute(pack, ('tm', 'state'), pairs + [(b, a) for a, b in pairs])  4.53 us
    ppermute x1, starting transfers between devices, per_device(): out_other = lax.ppermute(out, 'state', partner)  1.92 us
    ppermute x1, starting transfers between devices, per_device(): other_t = lax.ppermute(t_send, 'state', partner)  1.92 us
    ppermute x1, starting transfers between devices, per_device(): lax.ppermute(pack, ('tm', 'state'), pairs + [(b, a) for a, b in pairs])  1.92 us
    ppermute x1, waiting for transfers between devices, per_device(): out_other = lax.ppermute(out, 'state', partner)  1.36 us
  transfers between devices with their start and end apart: 4, of which 2 were waited for; matrix products, arithmetic and copies ran while one was open for 0% of the time, Pallas kernels for 6%

profile of v2, /device:TPU:1, one launch (start us, length us, event | category | flops | bytes accessed | tf_op | source)
XLA Modules:
  0.0 34.2 jit_solution(17144492115939064336)
XLA Ops:
  0.6 0.0 copy-start
  0.6 2.7 %shard_map.77 = (f32[4,72,128]{2,1,0:T(8,128)S(1)}, bf16[528,2048]{1,0:T(8,128)(2,1)S(1)}) custom-call(f32[64,512]{1,0:T(8,128)} %bitcast.1, f32[512,512]{1,0:T(8,128)} %means.1, f32[512,512]{1,0:T(8,128)} %precs.1, s32[4,16]{1,0:T(4,128)} %flags.1, bf16[512]{0:T(512)(128)(2,1)} %init.1), custom_call_target="tpu_custom_call" | custom-call | flops 1000000000 | bytes 1048576 | tf_op jit(solution)/shard_map/pallas_call | solution.py:300
  3.4 8.7 %collective-permute-start.1 = (bf16[528,2048]{1,0:T(8,128)(2,1)S(1)}, bf16[528,2048]{1,0:T(8,128)(2,1)S(1)}, u32[]{:S(2)}, u32[]{:S(2)}) collective-permute-start(bf16[528,2048]{1,0:T(8,128)(2,1)S(1)} %get-tuple-element.10.own_w), channel_id=1, source_target_pairs={{0,1},{1,0},{2,3},{3,2},{4,5},{5,4},{6,7},{7,6},{8,9},{9,8},{10,11... | collective-permute-start | bytes 6488072 | tf_op jit(solution)/shard_map/ppermute | solution.py:335
  12.1 0.0 copy-done
  12.1 0.5 %shard_map.80 = (bf16[512,1024]{1,0:T(8,128)(2,1)S(1)}, bf16[512,1024]{1,0:T(8,128)(2,1)S(1)}) custom-call(bf16[512,1024]{1,0:T(8,128)(2,1)S(1)} %copy-done), custom_call_target="tpu_custom_call" | custom-call | flops 1000000000 | bytes 1048576 | tf_op jit(solution)/shard_map/pallas_call | solution.py:300
  12.6 1.9 %collective-permute-start.2 = (bf16[512,1024]{1,0:T(8,128)(2,1)S(1)}, bf16[512,1024]{1,0:T(8,128)(2,1)S(1)}, u32[]{:S(2)}, u32[]{:S(2)}) collective-permute-start(bf16[512,1024]{1,0:T(8,128)(2,1)S(1)} %get-tuple-element.15), channel_id=1, source_target_pairs={{0,1},{1,0},{2,3},{3,2},{4,5},{5,4},{6,7},{7,6},{8,9},{9,8},{10,11... | collective-permute-start | bytes 3145736 | tf_op jit(solution)/shard_map/ppermute | solution.py:342
  14.5 1.9 %collective-permute-start = (f32[4,72,128]{2,1,0:T(8,128)S(1)}, f32[4,72,128]{2,1,0:T(8,128)S(1)}, u32[]{:S(2)}, u32[]{:S(2)}) collective-permute-start(f32[4,72,128]{2,1,0:T(8,128)S(1)} %get-tuple-element.9.own_pack), channel_id=1, source_target_pairs={{1,2},{3,4},{5,6},{7,8},{9,10},{11,12},{13,14},{15,16},{17,18},{19... | collective-permute-start | bytes 442376 | tf_op jit(solution)/shard_map/ppermute | solution.py:334
  16.5 4.5 %collective-permute-done.halo_pack = f32[4,72,128]{2,1,0:T(8,128)S(1)} collective-permute-done((f32[4,72,128]{2,1,0:T(8,128)S(1)}, f32[4,72,128]{2,1,0:T(8,128)S(1)}, u32[]{:S(2)}, u32[]{:S(2)}) %collective-permute-start) | collective-permute-done | bytes 147488 | tf_op jit(solution)/shard_map/ppermute | solution.py:334
  21.0 0.8 %shard_map.78 = (bf16[256,1024]{1,0:T(8,128)(2,1)S(1)}, f32[128,512]{1,0:T(8,128)S(1)}, f32[128,128]{1,0:T(8,128)S(1)}) custom-call(f32[4,72,128]{2,1,0:T(8,128)S(1)} %get-tuple-element.9.own_pack, f32[4,72,128]{2,1,0:T(8,128)S(1)} %collective-permute-done.halo_pack, bf16[528,2048]{1,0:T(8,128)(2,1)S(1)} %get-tuple-element.10.own_w), custom_call_target="tpu_custom_call" | custom-call | flops 1000000000 | bytes 1048576 | tf_op jit(solution)/shard_map/pallas_call | solution.py:300
  21.8 0.0 collective-permute-done.1.other_w
  21.8 0.9 %shard_map.79.emission = f32[128,1024]{1,0:T(8,128)S(1)} custom-call(bf16[256,1024]{1,0:T(8,128)(2,1)S(1)} %get-tuple-element.11.both, f32[128,512]{1,0:T(8,128)S(1)} %get-tuple-element.12.own_scores, bf16[528,2048]{1,0:T(8,128)(2,1)S(1)} %collective-permute-done.1.other_w), custom_call_target="tpu_custom_call" | custom-call | flops 1000000000 | bytes 1048576 | tf_op jit(solution)/shard_map/pallas_call | solution.py:300
  22.7 0.0 collective-permute-done.2.other_t
  22.7 7.5 %shard_map.81.own = bf16[64,1280]{1,0:T(8,128)(2,1)S(1)} custom-call(f32[128,1024]{1,0:T(8,128)S(1)} %shard_map.79.emission, f32[128,128]{1,0:T(8,128)S(1)} %get-tuple-element.13.place, bf16[528,2048]{1,0:T(8,128)(2,1)S(1)} %get-tuple-element.10.own_w, bf16[528,2048]{1,0:T(8,128)(2,1)S(1)} %collective-permute-done.1.other_w, ...), custom_call_target="tpu_custom_call" | custom-call | flops 10000000000 | bytes 1048576 | tf_op jit(solution)/shard_map/pallas_call | solution.py:300
  30.2 1.9 %collective-permute-start.3 = (bf16[64,1280]{1,0:T(8,128)(2,1)S(1)}, bf16[64,1280]{1,0:T(8,128)(2,1)S(1)}, u32[]{:S(2)}, u32[]{:S(2)}) collective-permute-start(bf16[64,1280]{1,0:T(8,128)(2,1)S(1)} %shard_map.81.own), channel_id=1, source_target_pairs={{0,1},{1,0},{2,3},{3,2},{4,5},{5,4},{6,7},{7,6},{8,9},{9,8},{10,11... | collective-permute-start | bytes 491528 | tf_op jit(solution)/shard_map/ppermute | solution.py:365
  32.1 1.4 %collective-permute-done.3.other = bf16[64,1280]{1,0:T(8,128)(2,1)S(1)} collective-permute-done((bf16[64,1280]{1,0:T(8,128)(2,1)S(1)}, bf16[64,1280]{1,0:T(8,128)(2,1)S(1)}, u32[]{:S(2)}, u32[]{:S(2)}) %collective-permute-start.3) | collective-permute-done | bytes 163872 | tf_op jit(solution)/shard_map/ppermute | solution.py:365
  33.5 0.8 %shard_map.82 = (bf16[4,16,512]{2,1,0:T(8,128)(2,1)}, f32[4,8]{1,0:T(4,128)}) custom-call(bf16[64,1280]{1,0:T(8,128)(2,1)S(1)} %shard_map.81.own, bf16[64,1280]{1,0:T(8,128)(2,1)S(1)} %collective-permute-done.3.other), custom_call_target="tpu_custom_call" | custom-call | flops 1000000 | bytes 1048576 | tf_op jit(solution)/shard_map/pallas_call | solution.py:300
Async XLA Ops:
  0.6 11.5 %copy-start = (bf16[512,1024]{1,0:T(8,128)(2,1)S(1)}, bf16[512,1024]{1,0:T(8,128)(2,1)}, u32[]{:S(2)}) copy-start(bf16[512,1024]{1,0:T(8,128)(2,1)} %trans.1) | copy-start | bytes 3145732
  3.4 18.4 %collective-permute-start.1 = (bf16[528,2048]{1,0:T(8,128)(2,1)S(1)}, bf16[528,2048]{1,0:T(8,128)(2,1)S(1)}, u32[]{:S(2)}, u32[]{:S(2)}) collective-permute-start(bf16[528,2048]{1,0:T(8,128)(2,1)S(1)} %get-tuple-element.10.own_w), channel_id=1, source_target_pairs={{0,1},{1,0},{2,3},{3,2},{4,5},{5,4},{6,7},{7,6},{8,9},{9,8},{10,11... | collective-permute-start | bytes 6488072 | tf_op jit(solution)/shard_map/ppermute | solution.py:335
  12.6 10.1 %collective-permute-start.2 = (bf16[512,1024]{1,0:T(8,128)(2,1)S(1)}, bf16[512,1024]{1,0:T(8,128)(2,1)S(1)}, u32[]{:S(2)}, u32[]{:S(2)}) collective-permute-start(bf16[512,1024]{1,0:T(8,128)(2,1)S(1)} %get-tuple-element.15), channel_id=1, source_target_pairs={{0,1},{1,0},{2,3},{3,2},{4,5},{5,4},{6,7},{7,6},{8,9},{9,8},{10,11... | collective-permute-start | bytes 3145736 | tf_op jit(solution)/shard_map/ppermute | solution.py:342
  14.5 6.5 %collective-permute-start = (f32[4,72,128]{2,1,0:T(8,128)S(1)}, f32[4,72,128]{2,1,0:T(8,128)S(1)}, u32[]{:S(2)}, u32[]{:S(2)}) collective-permute-start(f32[4,72,128]{2,1,0:T(8,128)S(1)} %get-tuple-element.9.own_pack), channel_id=1, source_target_pairs={{1,2},{3,4},{5,6},{7,8},{9,10},{11,12},{13,14},{15,16},{17,18},{19... | collective-permute-start | bytes 442376 | tf_op jit(solution)/shard_map/ppermute | solution.py:334
  30.2 3.3 %collective-permute-start.3 = (bf16[64,1280]{1,0:T(8,128)(2,1)S(1)}, bf16[64,1280]{1,0:T(8,128)(2,1)S(1)}, u32[]{:S(2)}, u32[]{:S(2)}) collective-permute-start(bf16[64,1280]{1,0:T(8,128)(2,1)S(1)} %shard_map.81.own), channel_id=1, source_target_pairs={{0,1},{1,0},{2,3},{3,2},{4,5},{5,4},{6,7},{7,6},{8,9},{9,8},{10,11... | collective-permute-start | bytes 491528 | tf_op jit(solution)/shard_map/ppermute | solution.py:365

commit v3 on v2

--- a/solution.py
+++ b/solution.py
@@ -10,8 +10,8 @@
 acoustic = 0.1
 VMEM = pltpu.VMEM
 MIB = 1 << 20
-CHUNKS = 4
 UNROLL = 3
+PARTS = 1
 SCALE = 2.0**108
 TRANSPOSED = (((1,), (1,)), ((), ()))
 bf16, f32 = jnp.bfloat16, jnp.float32
@@ -22,113 +22,122 @@
     return high, (x - high.astype(f32)).astype(bf16)
 
 
-def weights_kernel(
-    feats, means, precs, flags, init, pack, w_send, prec_in, mean_in, flag_in, init_in, sems
+def pair_columns(x):
+    x_hi, x_lo = split_pair(x)
+    q_hi, q_lo = split_pair(x * x)
+    high = jnp.concatenate([q_hi, x_hi], axis=1)
+    return jnp.concatenate([high, jnp.concatenate([q_lo, x_lo], axis=1)], axis=0)
+
+
+def some_scores(both, w_hi, w_lo, offset):
+    rows = both.shape[0] // 2
+    main = lax.dot_general(both, w_hi, TRANSPOSED, preferred_element_type=f32)
+    rest = lax.dot_general(both[0:rows], w_lo, TRANSPOSED, preferred_element_type=f32)
+    return main[0:rows] + (main[rows:] + rest) + offset
+
+
+def front_kernel(
+    feats, means, precs, flags, init, pack, w, offsets,
+    x_in, prec_in, mean_in, flag_in, init_in, sems,
 ):
     half, width = means.shape
     rows = feats.shape[0]
     streams, frames = flags.shape
-    step = half // CHUNKS
     pieces = width // 128
-    copies = []
-    for n in range(CHUNKS):
-        at = slice(n * step, (n + 1) * step)
-        copies.append(pltpu.make_async_copy(precs.at[at], prec_in.at[at], sems.at[2 * n]))
-        copies.append(pltpu.make_async_copy(means.at[at], mean_in.at[at], sems.at[2 * n + 1]))
-    for c in range(pieces):
-        part = feats.at[:, 128 * c : 128 * c + 128]
-        copies.append(
-            pltpu.make_async_copy(part, pack.at[c, 0:rows], sems.at[2 * CHUNKS + c])
-        )
-    copies.append(pltpu.make_async_copy(flags, flag_in, sems.at[2 * CHUNKS + pieces]))
-    copies.append(pltpu.make_async_copy(init, init_in, sems.at[2 * CHUNKS + pieces + 1]))
+    pairs = [(feats, x_in)]
+    for n in range(PARTS):
+        at = slice(n * half // PARTS, (n + 1) * half // PARTS)
+        pairs += [(precs.at[at], prec_in.at[at]), (means.at[at], mean_in.at[at])]
+    pairs += [(flags, flag_in), (init, init_in)]
+    copies = [pltpu.make_async_copy(*p, sems.at[n]) for n, p in enumerate(pairs)]
     for copy in copies:
         copy.start()
-
-    ones = jnp.ones((16, width), bf16)
-    for n in range(CHUNKS):
-        copies[2 * n].wait()
-        copies[2 * n + 1].wait()
-        r = n * step
-        at = slice(r, r + step)
+    for n in (0, -2, -1):
+        copies[n].wait()
+    x = x_in[...]
+    for c in range(pieces):
+        pack[c, 0:rows, :] = x[:, 128 * c : 128 * c + 128]
+    init_row = init_in[...].astype(f32).reshape(1, half)
+    for c in range(pieces):
+        pack[c, 2 * rows : 2 * rows + 8, :] = jnp.broadcast_to(
+            init_row[:, 128 * c : 128 * c + 128], (8, 128)
+        )
+    flags_float = flag_in[...].astype(f32)
+    pack[0, 2 * rows + 4 : 2 * rows + 4 + streams, 0:frames] = flags_float
+    pack[0, 2 * rows + 4 : 2 * rows + 4 + streams, frames : 2 * frames] = flags_float
+    both = pair_columns(x)
+    ones = jnp.ones((16, 128), bf16)
+
+    def prepare(n):
+        at = slice(n * 128, n * 128 + 128)
         prec = prec_in[at, :]
         mean = mean_in[at, :]
         scaled = prec * mean
         quad_hi, quad_lo = split_pair((-0.5 * acoustic) * prec)
         lin_hi, lin_lo = split_pair(acoustic * scaled)
-        w_send[at, 0:width] = quad_hi
-        w_send[at, width : 2 * width] = lin_hi
-        w_send[at, 2 * width : 3 * width] = quad_lo
-        w_send[at, 3 * width : 4 * width] = lin_lo
-        terms_hi, terms_lo = split_pair((0.5 * acoustic) * (jnp.log(prec) - scaled * mean))
-        offset = lax.dot_general(ones, terms_hi, TRANSPOSED, preferred_element_type=f32)
-        offset = offset + lax.dot_general(ones, terms_lo, TRANSPOSED, preferred_element_type=f32)
-        offset_hi, offset_lo = split_pair(offset)
-        w_send[half : half + 16, r : r + step] = offset_hi
-        w_send[half : half + 16, half + r : half + r + step] = offset_lo
-    for copy in copies[2 * CHUNKS :]:
-        copy.wait()
-    w_send[half : half + 16, 2 * half : 3 * half] = jnp.broadcast_to(
-        init_in[...].astype(f32).reshape(1, half), (16, half)
-    ).astype(bf16)
-    w_send[half : half + 16, 3 * half : 4 * half] = jnp.zeros((16, half), bf16)
-    flags_float = flag_in[...].astype(f32)
-    pack[0, rows : rows + 8, :] = jnp.zeros((8, 128), f32)
-    pack[0, rows + 4 : rows + 4 + streams, 0:frames] = flags_float
-    pack[0, rows + 4 : rows + 4 + streams, frames : 2 * frames] = flags_float
-
-
-def turn_kernel(trans, t_send, t_keep):
-    core = lax.axis_index("state")
-    half = trans.shape[0]
-    turned_0 = trans[:, 0:half].T
-    turned_1 = trans[:, half : 2 * half].T
-
-    @pl.when(core == 0)
+        w_hi = jnp.concatenate([quad_hi, lin_hi], axis=1)
+        w_lo = jnp.concatenate([quad_lo, lin_lo], axis=1)
+        w[at, 0 : 2 * width] = w_hi
+        w[at, 2 * width : 4 * width] = w_lo
+        squares = scaled * mean
+        product, total, logs = None, None, None
+        for c in range(pieces):
+            cols = slice(128 * c, 128 * c + 128)
+            product = prec[:, cols] if product is None else product * prec[:, cols]
+            total = squares[:, cols] if total is None else total + squares[:, cols]
+            if c % 4 == 3 or c == pieces - 1:
+                logs = jnp.log(product) if logs is None else logs + jnp.log(product)
+                product = None
+        return w_hi, w_lo, split_pair((0.5 * acoustic) * (logs - total))
+
+    def score(n, w_hi, w_lo, terms):
+        offset = sum(
+            lax.dot_general(ones, t, TRANSPOSED, preferred_element_type=f32) for t in terms
+        )
+        offsets[:, n * 128 : n * 128 + 128] = offset[0:8]
+        pack[n, rows : 2 * rows, :] = some_scores(both, w_hi, w_lo, offset[0:1])
+
+    tiles = half // 128
+    for part in range(PARTS):
+        copies[1 + 2 * part].wait()
+        copies[2 + 2 * part].wait()
+        for n in range(part * tiles // PARTS, (part + 1) * tiles // PARTS):
+            score(n, *prepare(n))
+
+
+def turn_kernel(own_t, other_t, own_turned, other_turned):
+    half = own_t.shape[0]
+
+    @pl.when(lax.axis_index("state") == 1)
     def _():
-        t_keep[...] = trans[...]
-        t_send[:, 0:half] = turned_1
-        t_send[:, half : 2 * half] = turned_0
-
-    @pl.when(core == 1)
-    def _():
-        t_send[...] = trans[...]
-        t_keep[:, 0:half] = turned_1
-        t_keep[:, half : 2 * half] = turned_0
-
-
-def half_scores(both, w):
-    width = w.shape[1] // 4
-    half = w.shape[0] - 16
-    rows = both.shape[0] // 2
-    main = lax.dot_general(
-        both[...], w[0:half, 0 : 2 * width], TRANSPOSED, preferred_element_type=f32
-    )
-    rest = lax.dot_general(
-        both[0:rows, :],
-        w[0:half, 2 * width : 4 * width],
-        TRANSPOSED,
-        preferred_element_type=f32,
-    )
-    extra = w[half : half + 1, 0 : 2 * half].astype(f32)
-    return main[0:rows] + (main[rows : 2 * rows] + rest) + (extra[:, 0:half] + extra[:, half:])
-
-
-def scores_kernel(own_pack, halo_pack, own_w, both, scores, place):
+        for source, target in ((own_t, own_turned), (other_t, other_turned)):
+            target[:, 0:half] = source[:, half : 2 * half].T
+            target[:, half : 2 * half] = source[:, 0:half].T
+
+
+def halo_kernel(own_pack, halo_pack, w, offsets, halo_scores, place):
     core = lax.axis_index("state")
     is_last = lax.axis_index("tm") == lax.axis_size("tm") - 1
     pieces = own_pack.shape[0]
     width = 128 * pieces
-    own_rows = own_pack.shape[1] - 8
-    rows = 2 * own_rows
-    frames = rows // 8
+    half = w.shape[0]
+    rows = (own_pack.shape[1] - 8) // 2
+    frames = rows // 4
+
+    x = jnp.concatenate([halo_pack[c, 0:rows, :] for c in range(pieces)], axis=1)
+    computed = some_scores(
+        pair_columns(x), w[:, 0 : 2 * width], w[:, 2 * width : 4 * width], offsets[0:1, :]
+    )
+    for c in range(half // 128):
+        halo_scores[c, :, :] = computed[:, 128 * c : 128 * c + 128]
 
     lane = lax.broadcasted_iota(jnp.int32, (4, 128), 1)
     end_reset = jnp.where((core == 1) & is_last, 1.0, 0.0)
+    flag_rows = slice(2 * rows + 4, 2 * rows + 8)
     flag4 = jnp.where(
         lane < frames,
-        jnp.maximum(halo_pack[0, own_rows + 4 : own_rows + 8, :], end_reset),
-        own_pack[0, own_rows + 4 : own_rows + 8, :],
+        jnp.maximum(halo_pack[0, flag_rows, :], end_reset),
+        own_pack[0, flag_rows, :],
     )
     flag4 = jnp.where(lane < 2 * frames, flag4, 0.0)
     flag8 = jnp.concatenate([flag4, flag4], axis=0)
@@ -143,37 +152,31 @@
         last = jnp.max(starts.astype(f32), axis=1, keepdims=True)
         place[8 * j : 8 * j + 8, :] = mine.astype(f32) - last
 
-    for c in range(pieces):
+
+def emission_kernel(own_pack, halo_pack, pair_pack, halo_scores, emission):
+    core = lax.axis_index("state")
+    rows = halo_scores.shape[1]
+    half = 128 * halo_scores.shape[0]
+    frames = rows // 4
+    for j in range(frames):
+        at = jnp.where(core == 0, j, frames - 1 - j)
         tiles = []
-        for j in range(frames):
-            at = jnp.where(core == 0, j, frames - 1 - j)
-            tiles.append(halo_pack[c, pl.ds(at, 4, stride=frames), :])
-            tiles.append(own_pack[c, pl.ds(at, 4, stride=frames), :])
-        x = jnp.concatenate(tiles, axis=0)
-        x_hi, x_lo = split_pair(x)
-        q_hi, q_lo = split_pair(x * x)
-        cols = slice(128 * c, 128 * c + 128)
-        past = slice(width + 128 * c, width + 128 * c + 128)
-        both[0:rows, cols] = q_hi
-        both[0:rows, past] = x_hi
-        both[rows : 2 * rows, cols] = q_lo
-        both[rows : 2 * rows, past] = x_lo
-    scores[...] = half_scores(both, own_w)
-
-
-def emission_kernel(both, own_scores, other_w, emission):
-    half = own_scores.shape[1]
-    other_scores = half_scores(both, other_w)
-    mine = own_scores[...]
-    top = jnp.maximum(
-        jnp.max(mine, axis=1, keepdims=True), jnp.max(other_scores, axis=1, keepdims=True)
-    )
-    emission[:, 0:half] = jnp.exp(mine - top)
-    emission[:, half : 2 * half] = jnp.exp(other_scores - top)
+        for near, far, first in ((halo_scores, own_pack, 0), (halo_pack, pair_pack, rows)):
+            for c in range(half // 128):
+                before = near[c, pl.ds(at + first, 4, stride=frames), :]
+                now = far[c, pl.ds(at + rows, 4, stride=frames), :]
+                tiles.append(jnp.concatenate([before, now], axis=0))
+        top = tiles[0]
+        for tile in tiles[1:]:
+            top = jnp.maximum(top, tile)
+        top = jnp.max(top, axis=1, keepdims=True)
+        for c, tile in enumerate(tiles):
+            emission[8 * j : 8 * j + 8, 128 * c : 128 * c + 128] = jnp.exp(tile - top)
 
 
 def chain_kernel(
-    emission, place, own_w, other_w, own_t, other_t, out, chain, done, part, gain, sums, gains, ordered
+    emission, place, own_pack, pair_pack, own_t, other_t, own_turned, other_turned,
+    out, chain, done, part, gain, sums, gains, ordered,
 ):
     core = lax.axis_index("state")
     half, states = own_t.shape
@@ -205,9 +208,9 @@
 
     def run(index):
         if index == 0:
-            line = slice(half, half + 1)
+            line = slice(own_pack.shape[1] - 8, own_pack.shape[1] - 7)
             first = jnp.concatenate(
-                [w[line, 2 * half : 3 * half].astype(f32) for w in (own_w, other_w)], axis=1
+                [p[c, line, :] for p in (own_pack, pair_pack) for c in range(half // 128)], axis=1
             )
             first = first / jnp.sum(first, axis=1, keepdims=True)
         else:
@@ -228,7 +231,8 @@
             if index == 0:
                 blocks = (own_t[:, 0:half], other_t[:, 0:half], own_t[:, half:], other_t[:, half:])
             else:
-                blocks = (own_t[:, 0:half], own_t[:, half:], other_t[:, 0:half], other_t[:, half:])
+                mine_t, other = own_turned, other_turned
+                blocks = (mine_t[:, 0:half], mine_t[:, half:], other[:, 0:half], other[:, half:])
             predicted = jnp.concatenate(
                 [
                     jnp.dot(mine, blocks[2 * n], preferred_element_type=f32)
@@ -316,15 +320,16 @@
     blocks = lax.axis_size("tm")
     partner = [(0, 1), (1, 0)]
 
-    pack, w_send = kernel(
-        weights_kernel,
-        [((width // 128, rows + 8, 128), f32), ((half + 16, 4 * width), bf16)],
+    pack, w, offsets = kernel(
+        front_kernel,
+        [((width // 128, 2 * rows + 8, 128), f32), ((half, 4 * width), bf16), ((8, half), f32)],
         [
+            VMEM((rows, width), f32),
             VMEM((half, width), f32),
             VMEM((half, width), f32),
             VMEM((streams, frames), jnp.int32),
             VMEM((half,), bf16),
-            pltpu.SemaphoreType.DMA((2 * CHUNKS + width // 128 + 2,)),
+            pltpu.SemaphoreType.DMA((2 * PARTS + 3,)),
         ],
         16, 10**9,
         features.reshape(rows, width), gauss_means, precisions, reset_flags, initial,
@@ -332,23 +337,23 @@
     )
     pairs = [(2 * i - 1, 2 * i) for i in range(1, blocks)]
     halo = lax.ppermute(pack, ("tm", "state"), pairs + [(b, a) for a, b in pairs])
-    other_w = lax.ppermute(w_send, "state", partner)
-    t_send, t_keep = kernel(
+    other_t = lax.ppermute(transitions, "state", partner)
+    pair = lax.ppermute(pack, "state", partner)
+    own_turned, other_turned = kernel(
         turn_kernel,
         [((half, states), bf16), ((half, states), bf16)],
         [], 16, 10**9,
-        transitions,
-    )
-    other_t = lax.ppermute(t_send, "state", partner)
-    both, scores, place = kernel(
-        scores_kernel,
-        [((4 * rows, 2 * width), bf16), ((2 * rows, half), f32), ((2 * rows, 128), f32)],
+        transitions, other_t,
+    )
+    halo_scores, place = kernel(
+        halo_kernel,
+        [((half // 128, rows, 128), f32), ((2 * rows, 128), f32)],
         [], 16, 10**9,
-        pack, halo, w_send,
+        pack, halo, w, offsets,
     )
     (emission,) = kernel(
         emission_kernel, [((2 * rows, states), f32)], [], 16, 10**9,
-        both, scores, other_w,
+        pack, halo, pair, halo_scores,
     )
     wide, narrow = VMEM((2 * rows, states), f32), VMEM((2 * rows, 128), f32)
     (out,) = kernel(
@@ -360,7 +365,7 @@
             VMEM((states // 128 + 1, rows, 128), f32),
         ],
         24, 10**10,
-        emission, place, w_send, other_w, t_keep, other_t,
+        emission, place, pack, pair, transitions, other_t, own_turned, other_turned,
     )
     out_other = lax.ppermute(out, "state", partner)
     posterior, evidence = kernel(

time: 34.4 us -> 34.4 us (level)
  local copies, waits for them, and re-layouts: 0.01 us -> 0.91 us
  waiting for transfers between devices: 5.9 us -> 5.38 us
  Pallas kernels: 13.1 us -> 12.7 us
    unnamed x2, local copies, waits for them, and re-layouts: 0.01 us -> 0.91 us
    ppermute x1, waiting for transfers between devices: 4.53 us -> 4.01 us  [per_device(): lax.ppermute(pack, ('tm', 'state'), pairs + [(b, a) for a, b in pairs])]
    pallas_call x6, Pallas kernels: 13.1 us -> 12.7 us  [kernel(): pl.pallas_call(body, out_shape=[jax.ShapeDtypeStruct(*o) for o in outs],...]
  transfers between devices with their start and end apart: 4 -> 4, of which waited for: 2 -> 2; matrix products, arithmetic and copies ran while one was open for 0% -> 0% of each run, Pallas kernels for 6% -> 11%
where the time goes in v3:
time: 34.4 us; the launch traced here: 34.2 us
  starting transfers between devices  14.5 us (42%)
  Pallas kernels  12.7 us (37%)
  waiting for transfers between devices  5.38 us (16%)
  local copies, waits for them, and re-layouts  0.91 us (3%)
  between operations  0.72 us (2%)
    pallas_call x6, Pallas kernels, kernel(): pl.pallas_call(body, out_shape=[jax.ShapeDtypeStruct(*o) for o in outs],...  12.7 us
    ppermute x1, starting transfers between devices, per_device(): other_t = lax.ppermute(transitions, 'state', partner)  8.75 us
    ppermute x1, waiting for transfers between devices, per_device(): lax.ppermute(pack, ('tm', 'state'), pairs + [(b, a) for a, b in pairs])  4.01 us
    ppermute x1, starting transfers between devices, per_device(): out_other = lax.ppermute(out, 'state', partner)  1.92 us
    ppermute x1, starting transfers between devices, per_device(): lax.ppermute(pack, ('tm', 'state'), pairs + [(b, a) for a, b in pairs])  1.92 us
    ppermute x1, starting transfers between devices, per_device(): pair = lax.ppermute(pack, 'state', partner)  1.92 us
    ppermute x1, waiting for transfers between devices, per_device(): out_other = lax.ppermute(out, 'state', partner)  1.36 us
    unnamed x2, local copies, waits for them, and re-layouts  0.91 us
  transfers between devices with their start and end apart: 4, of which 2 were waited for; matrix products, arithmetic and copies ran while one was open for 0% of the time, Pallas kernels for 11%

profile of v3, /device:TPU:1, one launch (start us, length us, event | category | flops | bytes accessed | tf_op | source)
XLA Modules:
  0.0 34.2 jit_solution(2702550483511272986)
XLA Ops:
  0.6 8.7 %collective-permute-start.2 = (bf16[512,1024]{1,0:T(8,128)(2,1)}, bf16[512,1024]{1,0:T(8,128)(2,1)S(1)}, u32[]{:S(2)}, u32[]{:S(2)}) collective-permute-start(bf16[512,1024]{1,0:T(8,128)(2,1)} %own_t.3), channel_id=1, source_target_pairs={{0,1},{1,0},{2,3},{3,2},{4,5},{5,4},{6,7},{7,6},{8,9},{9,8},{10,11... | collective-permute-start | bytes 3145736 | tf_op jit(solution)/shard_map/ppermute | solution.py:340
  9.4 2.7 %shard_map.77 = (f32[4,136,128]{2,1,0:T(8,128)S(1)}, bf16[512,2048]{1,0:T(8,128)(2,1)S(1)}, f32[8,512]{1,0:T(8,128)S(1)}) custom-call(f32[64,512]{1,0:T(8,128)} %bitcast.1, f32[512,512]{1,0:T(8,128)} %means.1, f32[512,512]{1,0:T(8,128)} %precs.1, s32[4,16]{1,0:T(4,128)} %flags.1, bf16[512]{0:T(512)(128)(2,1)} %init.1), custom_call_target="tpu_custom_call" | custom-call | flops 1000000000 | bytes 1048576 | tf_op jit(solution)/shard_map/pallas_call | solution.py:304
  12.1 1.9 %collective-permute-start = (f32[4,136,128]{2,1,0:T(8,128)S(1)}, f32[4,136,128]{2,1,0:T(8,128)S(1)}, u32[]{:S(2)}, u32[]{:S(2)}) collective-permute-start(f32[4,136,128]{2,1,0:T(8,128)S(1)} %get-tuple-element.9.own_pack), channel_id=1, source_target_pairs={{1,2},{3,4},{5,6},{7,8},{9,10},{11,12},{13,14},{15,16},{17,18},{19... | collective-permute-start | bytes 835592 | tf_op jit(solution)/shard_map/ppermute | solution.py:339
  14.1 1.9 %collective-permute-start.1 = (f32[4,136,128]{2,1,0:T(8,128)S(1)}, f32[4,136,128]{2,1,0:T(8,128)S(1)}, u32[]{:S(2)}, u32[]{:S(2)}) collective-permute-start(f32[4,136,128]{2,1,0:T(8,128)S(1)} %get-tuple-element.9.own_pack), channel_id=1, source_target_pairs={{0,1},{1,0},{2,3},{3,2},{4,5},{5,4},{6,7},{7,6},{8,9},{9,8},{10,11... | collective-permute-start | bytes 835592 | tf_op jit(solution)/shard_map/ppermute | solution.py:341
  16.0 4.0 %collective-permute-done.halo_pack = f32[4,136,128]{2,1,0:T(8,128)S(1)} collective-permute-done((f32[4,136,128]{2,1,0:T(8,128)S(1)}, f32[4,136,128]{2,1,0:T(8,128)S(1)}, u32[]{:S(2)}, u32[]{:S(2)}) %collective-permute-start) | collective-permute-done | bytes 278560 | tf_op jit(solution)/shard_map/ppermute | solution.py:339
  20.0 0.8 %shard_map.78 = (f32[4,64,128]{2,1,0:T(8,128)S(1)}, f32[128,128]{1,0:T(8,128)S(1)}) custom-call(f32[4,136,128]{2,1,0:T(8,128)S(1)} %get-tuple-element.9.own_pack, f32[4,136,128]{2,1,0:T(8,128)S(1)} %collective-permute-done.halo_pack, bf16[512,2048]{1,0:T(8,128)(2,1)S(1)} %get-tuple-element.10.w, f32[8,512]{1,0:T(8,128)S(1)} %get-tuple-element.11.offsets), custom_call_target="tpu_custom_call" | custom-call | flops 1000000000 | bytes 1048576 | tf_op jit(solution)/shard_map/pallas_call | solution.py:304
  20.8 0.0 copy-start
  20.8 0.0 collective-permute-done.1.pair_pack
  20.8 0.3 shard_map.79.emission
  21.1 0.0 collective-permute-done.2.other_t
  21.1 0.9 %copy-done = bf16[512,1024]{1,0:T(8,128)(2,1)S(1)} copy-done((bf16[512,1024]{1,0:T(8,128)(2,1)S(1)}, bf16[512,1024]{1,0:T(8,128)(2,1)}, u32[]{:S(2)}) %copy-start) | copy-done | bytes 1048600
  22.0 0.6 %shard_map.80 = (bf16[512,1024]{1,0:T(8,128)(2,1)S(1)}, bf16[512,1024]{1,0:T(8,128)(2,1)S(1)}) custom-call(bf16[512,1024]{1,0:T(8,128)(2,1)S(1)} %copy-done, bf16[512,1024]{1,0:T(8,128)(2,1)S(1)} %collective-permute-done.2.other_t), custom_call_target="tpu_custom_call" | custom-call | flops 1000000000 | bytes 1048576 | tf_op jit(solution)/shard_map/pallas_call | solution.py:304
  22.7 7.5 %shard_map.81.own = bf16[64,1280]{1,0:T(8,128)(2,1)S(1)} custom-call(f32[128,1024]{1,0:T(8,128)S(1)} %shard_map.79.emission, f32[128,128]{1,0:T(8,128)S(1)} %get-tuple-element.13.place, f32[4,136,128]{2,1,0:T(8,128)S(1)} %get-tuple-element.9.own_pack, f32[4,136,128]{2,1,0:T(8,128)S(1)} %collective-permute-done.1.pair_pack, bf16[512,1024]{1,0:T(8,128)(2,1)S(1)} %copy-done, ...), custom_call_target="tpu_custom_call" | custom-call | flops 10000000000 | bytes 1048576 | tf_op jit(solution)/shard_map/pallas_call | solution.py:304
  30.1 1.9 %collective-permute-start.3 = (bf16[64,1280]{1,0:T(8,128)(2,1)S(1)}, bf16[64,1280]{1,0:T(8,128)(2,1)S(1)}, u32[]{:S(2)}, u32[]{:S(2)}) collective-permute-start(bf16[64,1280]{1,0:T(8,128)(2,1)S(1)} %shard_map.81.own), channel_id=1, source_target_pairs={{0,1},{1,0},{2,3},{3,2},{4,5},{5,4},{6,7},{7,6},{8,9},{9,8},{10,11... | collective-permute-start | bytes 491528 | tf_op jit(solution)/shard_map/ppermute | solution.py:370
  32.1 1.4 %collective-permute-done.3.other = bf16[64,1280]{1,0:T(8,128)(2,1)S(1)} collective-permute-done((bf16[64,1280]{1,0:T(8,128)(2,1)S(1)}, bf16[64,1280]{1,0:T(8,128)(2,1)S(1)}, u32[]{:S(2)}, u32[]{:S(2)}) %collective-permute-start.3) | collective-permute-done | bytes 163872 | tf_op jit(solution)/shard_map/ppermute | solution.py:370
  33.4 0.8 %shard_map.82 = (bf16[4,16,512]{2,1,0:T(8,128)(2,1)}, f32[4,8]{1,0:T(4,128)}) custom-call(bf16[64,1280]{1,0:T(8,128)(2,1)S(1)} %shard_map.81.own, bf16[64,1280]{1,0:T(8,128)(2,1)S(1)} %collective-permute-done.3.other), custom_call_target="tpu_custom_call" | custom-call | flops 1000000 | bytes 1048576 | tf_op jit(solution)/shard_map/pallas_call | solution.py:304
Async XLA Ops:
  0.6 20.5 %collective-permute-start.2 = (bf16[512,1024]{1,0:T(8,128)(2,1)}, bf16[512,1024]{1,0:T(8,128)(2,1)S(1)}, u32[]{:S(2)}, u32[]{:S(2)}) collective-permute-start(bf16[512,1024]{1,0:T(8,128)(2,1)} %own_t.3), channel_id=1, source_target_pairs={{0,1},{1,0},{2,3},{3,2},{4,5},{5,4},{6,7},{7,6},{8,9},{9,8},{10,11... | collective-permute-start | bytes 3145736 | tf_op jit(solution)/shard_map/ppermute | solution.py:340
  12.1 7.9 %collective-permute-start = (f32[4,136,128]{2,1,0:T(8,128)S(1)}, f32[4,136,128]{2,1,0:T(8,128)S(1)}, u32[]{:S(2)}, u32[]{:S(2)}) collective-permute-start(f32[4,136,128]{2,1,0:T(8,128)S(1)} %get-tuple-element.9.own_pack), channel_id=1, source_target_pairs={{1,2},{3,4},{5,6},{7,8},{9,10},{11,12},{13,14},{15,16},{17,18},{19... | collective-permute-start | bytes 835592 | tf_op jit(solution)/shard_map/ppermute | solution.py:339
  14.1 6.7 %collective-permute-start.1 = (f32[4,136,128]{2,1,0:T(8,128)S(1)}, f32[4,136,128]{2,1,0:T(8,128)S(1)}, u32[]{:S(2)}, u32[]{:S(2)}) collective-permute-start(f32[4,136,128]{2,1,0:T(8,128)S(1)} %get-tuple-element.9.own_pack), channel_id=1, source_target_pairs={{0,1},{1,0},{2,3},{3,2},{4,5},{5,4},{6,7},{7,6},{8,9},{9,8},{10,11... | collective-permute-start | bytes 835592 | tf_op jit(solution)/shard_map/ppermute | solution.py:341
  20.8 1.2 %copy-start = (bf16[512,1024]{1,0:T(8,128)(2,1)S(1)}, bf16[512,1024]{1,0:T(8,128)(2,1)}, u32[]{:S(2)}) copy-start(bf16[512,1024]{1,0:T(8,128)(2,1)} %own_t.3) | copy-start | bytes 3145732
  30.1 3.3 %collective-permute-start.3 = (bf16[64,1280]{1,0:T(8,128)(2,1)S(1)}, bf16[64,1280]{1,0:T(8,128)(2,1)S(1)}, u32[]{:S(2)}, u32[]{:S(2)}) collective-permute-start(bf16[64,1280]{1,0:T(8,128)(2,1)S(1)} %shard_map.81.own), channel_id=1, source_target_pairs={{0,1},{1,0},{2,3},{3,2},{4,5},{5,4},{6,7},{7,6},{8,9},{9,8},{10,11... | collective-permute-start | bytes 491528 | tf_op jit(solution)/shard_map/ppermute | solution.py:370

commit v4 on v3

--- a/solution.py
+++ b/solution.py
@@ -31,14 +31,14 @@
 
 def some_scores(both, w_hi, w_lo, offset):
     rows = both.shape[0] // 2
-    main = lax.dot_general(both, w_hi, TRANSPOSED, preferred_element_type=f32)
-    rest = lax.dot_general(both[0:rows], w_lo, TRANSPOSED, preferred_element_type=f32)
+    main = jnp.dot(both, w_hi, preferred_element_type=f32)
+    rest = jnp.dot(both[0:rows], w_lo, preferred_element_type=f32)
     return main[0:rows] + (main[rows:] + rest) + offset
 
 
 def front_kernel(
-    feats, means, precs, flags, init, pack, w, offsets,
-    x_in, prec_in, mean_in, flag_in, init_in, sems,
+    feats, means, precs, flags, init, pack, scored, w, offsets,
+    extra, x_in, prec_in, mean_in, flag_in, init_in, sems,
 ):
     half, width = means.shape
     rows = feats.shape[0]
@@ -54,18 +54,14 @@
         copy.start()
     for n in (0, -2, -1):
         copies[n].wait()
-    x = x_in[...]
-    for c in range(pieces):
-        pack[c, 0:rows, :] = x[:, 128 * c : 128 * c + 128]
     init_row = init_in[...].astype(f32).reshape(1, half)
-    for c in range(pieces):
-        pack[c, 2 * rows : 2 * rows + 8, :] = jnp.broadcast_to(
+    for c in range(half // 128):
+        scored[c, rows : rows + 8, :] = jnp.broadcast_to(
             init_row[:, 128 * c : 128 * c + 128], (8, 128)
         )
-    flags_float = flag_in[...].astype(f32)
-    pack[0, 2 * rows + 4 : 2 * rows + 4 + streams, 0:frames] = flags_float
-    pack[0, 2 * rows + 4 : 2 * rows + 4 + streams, frames : 2 * frames] = flags_float
-    both = pair_columns(x)
+    both = pair_columns(x_in[...])
+    pack[:, 0:width] = both[0:rows, width : 2 * width]
+    pack[:, width : 2 * width] = both[rows : 2 * rows, width : 2 * width]
     ones = jnp.ones((16, 128), bf16)
 
     def prepare(n):
@@ -75,10 +71,10 @@
         scaled = prec * mean
         quad_hi, quad_lo = split_pair((-0.5 * acoustic) * prec)
         lin_hi, lin_lo = split_pair(acoustic * scaled)
-        w_hi = jnp.concatenate([quad_hi, lin_hi], axis=1)
-        w_lo = jnp.concatenate([quad_lo, lin_lo], axis=1)
-        w[at, 0 : 2 * width] = w_hi
-        w[at, 2 * width : 4 * width] = w_lo
+        w_hi = jnp.concatenate([quad_hi.T, lin_hi.T], axis=0)
+        w_lo = jnp.concatenate([quad_lo.T, lin_lo.T], axis=0)
+        w[:, at] = w_hi
+        w[:, half + n * 128 : half + n * 128 + 128] = w_lo
         squares = scaled * mean
         product, total, logs = None, None, None
         for c in range(pieces):
@@ -95,7 +91,7 @@
             lax.dot_general(ones, t, TRANSPOSED, preferred_element_type=f32) for t in terms
         )
         offsets[:, n * 128 : n * 128 + 128] = offset[0:8]
-        pack[n, rows : 2 * rows, :] = some_scores(both, w_hi, w_lo, offset[0:1])
+        scored[n, 0:rows, :] = some_scores(both, w_hi, w_lo, offset[0:1])
 
     tiles = half // 128
     for part in range(PARTS):
@@ -104,6 +100,27 @@
         for n in range(part * tiles // PARTS, (part + 1) * tiles // PARTS):
             score(n, *prepare(n))
 
+    top = scored[0, 0:rows, :]
+    for c in range(1, tiles):
+        top = jnp.maximum(top, scored[c, 0:rows, :])
+    top = jnp.max(top, axis=1, keepdims=True)
+    for c in range(tiles):
+        at = slice(2 * width + 128 * c, 2 * width + 128 * c + 128)
+        pack[:, at] = jnp.exp(scored[c, 0:rows, :] - top).astype(bf16)
+    extra[...] = jnp.zeros_like(extra)
+    flags_float = flag_in[...].astype(f32)
+    for b in range(streams):
+        line = jnp.broadcast_to(flags_float[b : b + 1, :], (frames, frames))
+        extra[b * frames : (b + 1) * frames, 0:frames] = line
+        extra[b * frames : (b + 1) * frames, frames : 2 * frames] = line
+    top_hi = top.astype(bf16)
+    extra[:, 2 * frames : 2 * frames + 1] = top_hi.astype(f32)
+    rest = top - top_hi.astype(f32)
+    rest_hi, rest_lo = split_pair(rest)
+    extra[:, 2 * frames + 1 : 2 * frames + 2] = rest_hi.astype(f32)
+    extra[:, 2 * frames + 2 : 2 * frames + 3] = rest_lo.astype(f32)
+    pack[:, 2 * width + half : 2 * width + half + 128] = extra[...].astype(bf16)
+
 
 def turn_kernel(own_t, other_t, own_turned, other_turned):
     half = own_t.shape[0]
@@ -115,30 +132,37 @@
             target[:, half : 2 * half] = source[:, 0:half].T
 
 
-def halo_kernel(own_pack, halo_pack, w, offsets, halo_scores, place):
+def halo_kernel(own_pack, halo_pack, w, offsets, halo_scores, far_scores, place):
     core = lax.axis_index("state")
     is_last = lax.axis_index("tm") == lax.axis_size("tm") - 1
-    pieces = own_pack.shape[0]
-    width = 128 * pieces
-    half = w.shape[0]
-    rows = (own_pack.shape[1] - 8) // 2
+    width = w.shape[0] // 2
+    half = w.shape[1] // 2
+    rows = own_pack.shape[0]
     frames = rows // 4
-
-    x = jnp.concatenate([halo_pack[c, 0:rows, :] for c in range(pieces)], axis=1)
-    computed = some_scores(
-        pair_columns(x), w[:, 0 : 2 * width], w[:, 2 * width : 4 * width], offsets[0:1, :]
-    )
+    side = slice(2 * width + half, 2 * width + half + 128)
+
+    x_hi, x_lo = halo_pack[:, 0:width], halo_pack[:, width : 2 * width]
+    x = x_hi.astype(f32) + x_lo.astype(f32)
+    q_hi, q_lo = split_pair(x * x)
+    both = jnp.concatenate(
+        [jnp.concatenate([q_hi, x_hi], axis=1), jnp.concatenate([q_lo, x_lo], axis=1)], axis=0
+    )
+    computed = some_scores(both, w[:, 0:half], w[:, half : 2 * half], offsets[0:1, :])
+    halo_side = halo_pack[:, side].astype(f32)
+    own_side = own_pack[:, side].astype(f32)
+    spot = lax.broadcasted_iota(jnp.int32, (rows, 128), 1) - 2 * frames
+    top = jnp.sum(jnp.where((spot >= 0) & (spot < 3), halo_side, 0.0), axis=1, keepdims=True)
     for c in range(half // 128):
-        halo_scores[c, :, :] = computed[:, 128 * c : 128 * c + 128]
+        at = slice(128 * c, 128 * c + 128)
+        halo_scores[c, :, :] = computed[:, at]
+        sent = halo_pack[:, 2 * width + 128 * c : 2 * width + 128 * c + 128].astype(f32)
+        far_scores[c, :, :] = top + jnp.log(sent)
 
     lane = lax.broadcasted_iota(jnp.int32, (4, 128), 1)
     end_reset = jnp.where((core == 1) & is_last, 1.0, 0.0)
-    flag_rows = slice(2 * rows + 4, 2 * rows + 8)
-    flag4 = jnp.where(
-        lane < frames,
-        jnp.maximum(halo_pack[0, flag_rows, :], end_reset),
-        own_pack[0, flag_rows, :],
-    )
+    halo_flags = jnp.concatenate([halo_side[b : b + 1] for b in range(0, rows, frames)], axis=0)
+    own_flags = jnp.concatenate([own_side[b : b + 1] for b in range(0, rows, frames)], axis=0)
+    flag4 = jnp.where(lane < frames, jnp.maximum(halo_flags, end_reset), own_flags)
     flag4 = jnp.where(lane < 2 * frames, flag4, 0.0)
     flag8 = jnp.concatenate([flag4, flag4], axis=0)
     lane8 = lax.broadcasted_iota(jnp.int32, (8, 128), 1)
@@ -153,7 +177,7 @@
         place[8 * j : 8 * j + 8, :] = mine.astype(f32) - last
 
 
-def emission_kernel(own_pack, halo_pack, pair_pack, halo_scores, emission):
+def emission_kernel(own_scores, far_scores, pair_scores, halo_scores, emission):
     core = lax.axis_index("state")
     rows = halo_scores.shape[1]
     half = 128 * halo_scores.shape[0]
@@ -161,10 +185,10 @@
     for j in range(frames):
         at = jnp.where(core == 0, j, frames - 1 - j)
         tiles = []
-        for near, far, first in ((halo_scores, own_pack, 0), (halo_pack, pair_pack, rows)):
+        for near, far in ((halo_scores, own_scores), (far_scores, pair_scores)):
             for c in range(half // 128):
-                before = near[c, pl.ds(at + first, 4, stride=frames), :]
-                now = far[c, pl.ds(at + rows, 4, stride=frames), :]
+                before = near[c, pl.ds(at, 4, stride=frames), :]
+                now = far[c, pl.ds(at, 4, stride=frames), :]
                 tiles.append(jnp.concatenate([before, now], axis=0))
         top = tiles[0]
         for tile in tiles[1:]:
@@ -175,13 +199,14 @@
 
 
 def chain_kernel(
-    emission, place, own_pack, pair_pack, own_t, other_t, own_turned, other_turned,
+    emission, place, own_scores, pair_scores, own_t, other_t, own_turned, other_turned,
     out, chain, done, part, gain, sums, gains, ordered,
 ):
     core = lax.axis_index("state")
     half, states = own_t.shape
     rows = place.shape[0]
     frames = rows // 8
+    own_rows = rows // 2
     shape = (rows, 128)
 
     def advance(x):
@@ -208,9 +233,9 @@
 
     def run(index):
         if index == 0:
-            line = slice(own_pack.shape[1] - 8, own_pack.shape[1] - 7)
+            line = slice(own_rows, own_rows + 1)
             first = jnp.concatenate(
-                [p[c, line, :] for p in (own_pack, pair_pack) for c in range(half // 128)], axis=1
+                [p[c, line, :] for p in (own_scores, pair_scores) for c in range(half // 128)], axis=1
             )
             first = first / jnp.sum(first, axis=1, keepdims=True)
         else:
@@ -320,10 +345,16 @@
     blocks = lax.axis_size("tm")
     partner = [(0, 1), (1, 0)]
 
-    pack, w, offsets = kernel(
+    pack, scored, w, offsets = kernel(
         front_kernel,
-        [((width // 128, 2 * rows + 8, 128), f32), ((half, 4 * width), bf16), ((8, half), f32)],
         [
+            ((rows, 2 * width + half + 128), bf16),
+            ((half // 128, rows + 8, 128), f32),
+            ((2 * width, 2 * half), bf16),
+            ((8, half), f32),
+        ],
+        [
+            VMEM((rows, 128), f32),
             VMEM((rows, width), f32),
             VMEM((half, width), f32),
             VMEM((half, width), f32),
@@ -338,22 +369,22 @@
     pairs = [(2 * i - 1, 2 * i) for i in range(1, blocks)]
     halo = lax.ppermute(pack, ("tm", "state"), pairs + [(b, a) for a, b in pairs])
     other_t = lax.ppermute(transitions, "state", partner)
-    pair = lax.ppermute(pack, "state", partner)
+    pair = lax.ppermute(scored, "state", partner)
     own_turned, other_turned = kernel(
         turn_kernel,
         [((half, states), bf16), ((half, states), bf16)],
         [], 16, 10**9,
         transitions, other_t,
     )
-    halo_scores, place = kernel(
+    halo_scores, far_scores, place = kernel(
         halo_kernel,
-        [((half // 128, rows, 128), f32), ((2 * rows, 128), f32)],
+        [((half // 128, rows, 128), f32)] * 2 + [((2 * rows, 128), f32)],
         [], 16, 10**9,
         pack, halo, w, offsets,
     )
     (emission,) = kernel(
         emission_kernel, [((2 * rows, states), f32)], [], 16, 10**9,
-        pack, halo, pair, halo_scores,
+        scored, far_scores, pair, halo_scores,
     )
     wide, narrow = VMEM((2 * rows, states), f32), VMEM((2 * rows, 128), f32)
     (out,) = kernel(
@@ -365,7 +396,7 @@
             VMEM((states // 128 + 1, rows, 128), f32),
         ],
         24, 10**10,
-        emission, place, pack, pair, transitions, other_t, own_turned, other_turned,
+        emission, place, scored, pair, transitions, other_t, own_turned, other_turned,
     )
     out_other = lax.ppermute(out, "state", partner)
     posterior, evidence = kernel(

time: 34.4 us -> 33.6 us (0.977)
  waiting for transfers between devices: 5.38 us -> 4.67 us
    ppermute x1, waiting for transfers between devices: 4.01 us -> 3.31 us  [per_device(): lax.ppermute(pack, ('tm', 'state'), pairs + [(b, a) for a, b in pairs])]
where the time goes in v4:
time: 33.6 us; the launch traced here: 33.3 us
  starting transfers between devices  14.5 us (43%)
  Pallas kernels  12.5 us (37%)
  waiting for transfers between devices  4.67 us (14%)
  local copies, waits for them, and re-layouts  0.89 us (3%)
  between operations  0.72 us (2%)
    pallas_call x6, Pallas kernels, kernel(): pl.pallas_call(body, out_shape=[jax.ShapeDtypeStruct(*o) for o in outs],...  12.5 us
    ppermute x1, starting transfers between devices, per_device(): other_t = lax.ppermute(transitions, 'state', partner)  8.75 us
    ppermute x1, waiting for transfers between devices, per_device(): lax.ppermute(pack, ('tm', 'state'), pairs + [(b, a) for a, b in pairs])  3.31 us
    ppermute x1, starting transfers between devices, per_device(): pair = lax.ppermute(scored, 'state', partner)  1.92 us
    ppermute x1, starting transfers between devices, per_device(): out_other = lax.ppermute(out, 'state', partner)  1.92 us
    ppermute x1, starting transfers between devices, per_device(): lax.ppermute(pack, ('tm', 'state'), pairs + [(b, a) for a, b in pairs])  1.92 us
    ppermute x1, waiting for transfers between devices, per_device(): out_other = lax.ppermute(out, 'state', partner)  1.36 us
    unnamed x2, local copies, waits for them, and re-layouts  0.89 us
  transfers between devices with their start and end apart: 4, of which 2 were waited for; matrix products, arithmetic and copies ran while one was open for 0% of the time, Pallas kernels for 11%

profile of v4, /device:TPU:1, one launch (start us, length us, event | category | flops | bytes accessed | tf_op | source)
XLA Modules:
  0.0 33.3 jit_solution(9178965957132546711)
XLA Ops:
  0.6 8.7 %collective-permute-start.2 = (bf16[512,1024]{1,0:T(8,128)(2,1)}, bf16[512,1024]{1,0:T(8,128)(2,1)S(1)}, u32[]{:S(2)}, u32[]{:S(2)}) collective-permute-start(bf16[512,1024]{1,0:T(8,128)(2,1)} %own_t.3), channel_id=1, source_target_pairs={{0,1},{1,0},{2,3},{3,2},{4,5},{5,4},{6,7},{7,6},{8,9},{9,8},{10,11... | collective-permute-start | bytes 3145736 | tf_op jit(solution)/shard_map/ppermute | solution.py:371
  9.4 2.9 %shard_map.77 = (bf16[64,1664]{1,0:T(8,128)(2,1)S(1)}, f32[4,72,128]{2,1,0:T(8,128)S(1)}, bf16[1024,1024]{1,0:T(8,128)(2,1)S(1)}, f32[8,512]{1,0:T(8,128)S(1)}) custom-call(f32[64,512]{1,0:T(8,128)} %bitcast.1, f32[512,512]{1,0:T(8,128)} %means.1, f32[512,512]{1,0:T(8,128)} %precs.1, s32[4,16]{1,0:T(4,128)} %flags.1, bf16[512]{0:T(512)(128)(2,1)} %init.1), custom_call_target="tpu_custom_call" | custom-call | flops 1000000000 | bytes 1048576 | tf_op jit(solution)/shard_map/pallas_call | solution.py:329
  12.3 1.9 %collective-permute-start = (bf16[64,1664]{1,0:T(8,128)(2,1)S(1)}, bf16[64,1664]{1,0:T(8,128)(2,1)S(1)}, u32[]{:S(2)}, u32[]{:S(2)}) collective-permute-start(bf16[64,1664]{1,0:T(8,128)(2,1)S(1)} %get-tuple-element.12.own_pack), channel_id=1, source_target_pairs={{1,2},{3,4},{5,6},{7,8},{9,10},{11,12},{13,14},{15,16},{17,18},{19... | collective-permute-start | bytes 638984 | tf_op jit(solution)/shard_map/ppermute | solution.py:370
  14.2 1.9 %collective-permute-start.1 = (f32[4,72,128]{2,1,0:T(8,128)S(1)}, f32[4,72,128]{2,1,0:T(8,128)S(1)}, u32[]{:S(2)}, u32[]{:S(2)}) collective-permute-start(f32[4,72,128]{2,1,0:T(8,128)S(1)} %get-tuple-element.11.own_scores), channel_id=1, source_target_pairs={{0,1},{1,0},{2,3},{3,2},{4,5},{5,4},{6,7},{7,6},{8,9},{9,8},{10,11... | collective-permute-start | bytes 442376 | tf_op jit(solution)/shard_map/ppermute | solution.py:372
  16.2 3.3 %collective-permute-done.halo_pack = bf16[64,1664]{1,0:T(8,128)(2,1)S(1)} collective-permute-done((bf16[64,1664]{1,0:T(8,128)(2,1)S(1)}, bf16[64,1664]{1,0:T(8,128)(2,1)S(1)}, u32[]{:S(2)}, u32[]{:S(2)}) %collective-permute-start) | collective-permute-done | bytes 213024 | tf_op jit(solution)/shard_map/ppermute | solution.py:370
  19.5 0.5 %shard_map.78 = (f32[4,64,128]{2,1,0:T(8,128)S(1)}, f32[4,64,128]{2,1,0:T(8,128)S(1)}, f32[128,128]{1,0:T(8,128)S(1)}) custom-call(bf16[64,1664]{1,0:T(8,128)(2,1)S(1)} %get-tuple-element.12.own_pack, bf16[64,1664]{1,0:T(8,128)(2,1)S(1)} %collective-permute-done.halo_pack, bf16[1024,1024]{1,0:T(8,128)(2,1)S(1)} %get-tuple-element.13.w, ...), custom_call_target="tpu_custom_call" | custom-call | flops 1000000000 | bytes 1048576 | tf_op jit(solution)/shard_map/pallas_call | solution.py:329
  19.9 0.0 copy-start
  19.9 0.0 collective-permute-done.1.pair_scores
  20.0 0.3 shard_map.79.emission
  20.3 0.0 collective-permute-done.2.other_t
  20.3 0.9 %copy-done = bf16[512,1024]{1,0:T(8,128)(2,1)S(1)} copy-done((bf16[512,1024]{1,0:T(8,128)(2,1)S(1)}, bf16[512,1024]{1,0:T(8,128)(2,1)}, u32[]{:S(2)}) %copy-start) | copy-done | bytes 1048600
  21.2 0.6 %shard_map.80 = (bf16[512,1024]{1,0:T(8,128)(2,1)S(1)}, bf16[512,1024]{1,0:T(8,128)(2,1)S(1)}) custom-call(bf16[512,1024]{1,0:T(8,128)(2,1)S(1)} %copy-done, bf16[512,1024]{1,0:T(8,128)(2,1)S(1)} %collective-permute-done.2.other_t), custom_call_target="tpu_custom_call" | custom-call | flops 1000000000 | bytes 1048576 | tf_op jit(solution)/shard_map/pallas_call | solution.py:329
  21.8 7.5 %shard_map.81.own = bf16[64,1280]{1,0:T(8,128)(2,1)S(1)} custom-call(f32[128,1024]{1,0:T(8,128)S(1)} %shard_map.79.emission, f32[128,128]{1,0:T(8,128)S(1)} %get-tuple-element.17.place, f32[4,72,128]{2,1,0:T(8,128)S(1)} %get-tuple-element.11.own_scores, f32[4,72,128]{2,1,0:T(8,128)S(1)} %collective-permute-done.1.pair_scores, bf16[512,1024]{1,0:T(8,128)(2,1)S(1)} %copy-done, ...), custom_call_target="tpu_custom_call" | custom-call | flops 10000000000 | bytes 1048576 | tf_op jit(solution)/shard_map/pallas_call | solution.py:329
  29.3 1.9 %collective-permute-start.3 = (bf16[64,1280]{1,0:T(8,128)(2,1)S(1)}, bf16[64,1280]{1,0:T(8,128)(2,1)S(1)}, u32[]{:S(2)}, u32[]{:S(2)}) collective-permute-start(bf16[64,1280]{1,0:T(8,128)(2,1)S(1)} %shard_map.81.own), channel_id=1, source_target_pairs={{0,1},{1,0},{2,3},{3,2},{4,5},{5,4},{6,7},{7,6},{8,9},{9,8},{10,11... | collective-permute-start | bytes 491528 | tf_op jit(solution)/shard_map/ppermute | solution.py:401
  31.2 1.4 %collective-permute-done.3.other = bf16[64,1280]{1,0:T(8,128)(2,1)S(1)} collective-permute-done((bf16[64,1280]{1,0:T(8,128)(2,1)S(1)}, bf16[64,1280]{1,0:T(8,128)(2,1)S(1)}, u32[]{:S(2)}, u32[]{:S(2)}) %collective-permute-start.3) | collective-permute-done | bytes 163872 | tf_op jit(solution)/shard_map/ppermute | solution.py:401
  32.6 0.8 %shard_map.82 = (bf16[4,16,512]{2,1,0:T(8,128)(2,1)}, f32[4,8]{1,0:T(4,128)}) custom-call(bf16[64,1280]{1,0:T(8,128)(2,1)S(1)} %shard_map.81.own, bf16[64,1280]{1,0:T(8,128)(2,1)S(1)} %collective-permute-done.3.other), custom_call_target="tpu_custom_call" | custom-call | flops 1000000 | bytes 1048576 | tf_op jit(solution)/shard_map/pallas_call | solution.py:329
Async XLA Ops:
  0.6 19.6 %collective-permute-start.2 = (bf16[512,1024]{1,0:T(8,128)(2,1)}, bf16[512,1024]{1,0:T(8,128)(2,1)S(1)}, u32[]{:S(2)}, u32[]{:S(2)}) collective-permute-start(bf16[512,1024]{1,0:T(8,128)(2,1)} %own_t.3), channel_id=1, source_target_pairs={{0,1},{1,0},{2,3},{3,2},{4,5},{5,4},{6,7},{7,6},{8,9},{9,8},{10,11... | collective-permute-start | bytes 3145736 | tf_op jit(solution)/shard_map/ppermute | solution.py:371
  12.3 7.2 %collective-permute-start = (bf16[64,1664]{1,0:T(8,128)(2,1)S(1)}, bf16[64,1664]{1,0:T(8,128)(2,1)S(1)}, u32[]{:S(2)}, u32[]{:S(2)}) collective-permute-start(bf16[64,1664]{1,0:T(8,128)(2,1)S(1)} %get-tuple-element.12.own_pack), channel_id=1, source_target_pairs={{1,2},{3,4},{5,6},{7,8},{9,10},{11,12},{13,14},{15,16},{17,18},{19... | collective-permute-start | bytes 638984 | tf_op jit(solution)/shard_map/ppermute | solution.py:370
  14.2 5.7 %collective-permute-start.1 = (f32[4,72,128]{2,1,0:T(8,128)S(1)}, f32[4,72,128]{2,1,0:T(8,128)S(1)}, u32[]{:S(2)}, u32[]{:S(2)}) collective-permute-start(f32[4,72,128]{2,1,0:T(8,128)S(1)} %get-tuple-element.11.own_scores), channel_id=1, source_target_pairs={{0,1},{1,0},{2,3},{3,2},{4,5},{5,4},{6,7},{7,6},{8,9},{9,8},{10,11... | collective-permute-start | bytes 442376 | tf_op jit(solution)/shard_map/ppermute | solution.py:372
  19.9 1.2 %copy-start = (bf16[512,1024]{1,0:T(8,128)(2,1)S(1)}, bf16[512,1024]{1,0:T(8,128)(2,1)}, u32[]{:S(2)}) copy-start(bf16[512,1024]{1,0:T(8,128)(2,1)} %own_t.3) | copy-start | bytes 3145732
  29.3 3.3 %collective-permute-start.3 = (bf16[64,1280]{1,0:T(8,128)(2,1)S(1)}, bf16[64,1280]{1,0:T(8,128)(2,1)S(1)}, u32[]{:S(2)}, u32[]{:S(2)}) collective-permute-start(bf16[64,1280]{1,0:T(8,128)(2,1)S(1)} %shard_map.81.own), channel_id=1, source_target_pairs={{0,1},{1,0},{2,3},{3,2},{4,5},{5,4},{6,7},{7,6},{8,9},{9,8},{10,11... | collective-permute-start | bytes 491528 | tf_op jit(solution)/shard_map/ppermute | solution.py:401

commit v5 on v4

--- a/solution.py
+++ b/solution.py
@@ -11,7 +11,7 @@
 VMEM = pltpu.VMEM
 MIB = 1 << 20
 UNROLL = 3
-PARTS = 1
+PARTS = 2
 SCALE = 2.0**108
 TRANSPOSED = (((1,), (1,)), ((), ()))
 bf16, f32 = jnp.bfloat16, jnp.float32
@@ -22,9 +22,9 @@
     return high, (x - high.astype(f32)).astype(bf16)
 
 
-def pair_columns(x):
-    x_hi, x_lo = split_pair(x)
-    q_hi, q_lo = split_pair(x * x)
+def pair_columns(x_hi, x_lo):
+    x = x_hi.astype(f32) + x_lo.astype(f32)
+    q_hi, q_lo = split_pair((-0.5 / acoustic) * (x * x))
     high = jnp.concatenate([q_hi, x_hi], axis=1)
     return jnp.concatenate([high, jnp.concatenate([q_lo, x_lo], axis=1)], axis=0)
 
@@ -59,9 +59,10 @@
         scored[c, rows : rows + 8, :] = jnp.broadcast_to(
             init_row[:, 128 * c : 128 * c + 128], (8, 128)
         )
-    both = pair_columns(x_in[...])
-    pack[:, 0:width] = both[0:rows, width : 2 * width]
-    pack[:, width : 2 * width] = both[rows : 2 * rows, width : 2 * width]
+    x_hi, x_lo = split_pair(acoustic * x_in[...])
+    pack[:, 0:width] = x_hi
+    pack[:, width : 2 * width] = x_lo
+    both = pair_columns(x_hi, x_lo)
     ones = jnp.ones((16, 128), bf16)
 
     def prepare(n):
@@ -69,8 +70,8 @@
         prec = prec_in[at, :]
         mean = mean_in[at, :]
         scaled = prec * mean
-        quad_hi, quad_lo = split_pair((-0.5 * acoustic) * prec)
-        lin_hi, lin_lo = split_pair(acoustic * scaled)
+        quad_hi, quad_lo = split_pair(prec)
+        lin_hi, lin_lo = split_pair(scaled)
         w_hi = jnp.concatenate([quad_hi.T, lin_hi.T], axis=0)
         w_lo = jnp.concatenate([quad_lo.T, lin_lo.T], axis=0)
         w[:, at] = w_hi
@@ -122,14 +123,13 @@
     pack[:, 2 * width + half : 2 * width + half + 128] = extra[...].astype(bf16)
 
 
-def turn_kernel(own_t, other_t, own_turned, other_turned):
-    half = own_t.shape[0]
+def turn_kernel(source, turned):
+    half = source.shape[0]
 
     @pl.when(lax.axis_index("state") == 1)
     def _():
-        for source, target in ((own_t, own_turned), (other_t, other_turned)):
-            target[:, 0:half] = source[:, half : 2 * half].T
-            target[:, half : 2 * half] = source[:, 0:half].T
+        turned[:, 0:half] = source[:, half : 2 * half].T
+        turned[:, half : 2 * half] = source[:, 0:half].T
 
 
 def halo_kernel(own_pack, halo_pack, w, offsets, halo_scores, far_scores, place):
@@ -141,12 +141,7 @@
     frames = rows // 4
     side = slice(2 * width + half, 2 * width + half + 128)
 
-    x_hi, x_lo = halo_pack[:, 0:width], halo_pack[:, width : 2 * width]
-    x = x_hi.astype(f32) + x_lo.astype(f32)
-    q_hi, q_lo = split_pair(x * x)
-    both = jnp.concatenate(
-        [jnp.concatenate([q_hi, x_hi], axis=1), jnp.concatenate([q_lo, x_lo], axis=1)], axis=0
-    )
+    both = pair_columns(halo_pack[:, 0:width], halo_pack[:, width : 2 * width])
     computed = some_scores(both, w[:, 0:half], w[:, half : 2 * half], offsets[0:1, :])
     halo_side = halo_pack[:, side].astype(f32)
     own_side = own_pack[:, side].astype(f32)
@@ -218,7 +213,7 @@
         sums[...] = jnp.where(place[...] == k - 1.0, total, sums[...])
         return total
 
-    def spread(k, predicted, scale, index):
+    def spread(k, predicted, scale, index, first=False):
         mask = place[...] == k
         sum_tile = None
         for c in range(states // 128):
@@ -227,7 +222,7 @@
             weighted = ahead * emission[:, at]
             sum_tile = weighted if sum_tile is None else sum_tile + weighted
             result = weighted if index == 0 else ahead
-            done[:, at] = jnp.where(mask, result, done[:, at])
+            done[:, at] = result if first else jnp.where(mask, result, done[:, at])
             chain[:, at] = advance(weighted * scale).astype(bf16)
         part[...] = sum_tile
 
@@ -243,8 +238,7 @@
         gain[...] = jnp.full(shape, SCALE, f32)
         gains[...] = jnp.full(shape, SCALE, f32)
         sums[...] = jnp.full(shape, SCALE, f32)
-        done[...] = jnp.zeros_like(done)
-        spread(0.0, jnp.broadcast_to(first, (rows, states)), SCALE, index)
+        spread(0.0, jnp.broadcast_to(first, (rows, states)), SCALE, index, True)
 
         def step(k, carry):
             k = k.astype(f32)
@@ -370,12 +364,9 @@
     halo = lax.ppermute(pack, ("tm", "state"), pairs + [(b, a) for a, b in pairs])
     other_t = lax.ppermute(transitions, "state", partner)
     pair = lax.ppermute(scored, "state", partner)
-    own_turned, other_turned = kernel(
-        turn_kernel,
-        [((half, states), bf16), ((half, states), bf16)],
-        [], 16, 10**9,
-        transitions, other_t,
-    )
+    block = [((half, states), bf16)]
+    (own_turned,) = kernel(turn_kernel, block, [], 16, 10**9, transitions)
+    (other_turned,) = kernel(turn_kernel, block, [], 16, 10**9, other_t)
     halo_scores, far_scores, place = kernel(
         halo_kernel,
         [((half // 128, rows, 128), f32)] * 2 + [((2 * rows, 128), f32)],

time: 33.6 us -> 32.4 us (0.964)
  local copies, waits for them, and re-layouts: 0.89 us -> 0.01 us
  waiting for transfers between devices: 4.67 us -> 4.31 us
    unnamed x2, local copies, waits for them, and re-layouts: 0.89 us -> 0.01 us
    ppermute x1, waiting for transfers between devices: 3.31 us -> 2.94 us  [per_device(): lax.ppermute(pack, ('tm', 'state'), pairs + [(b, a) for a, b in pairs])]
    pallas_call x6 -> x7, Pallas kernels: 12.5 us -> 12.5 us  [kernel(): pl.pallas_call(body, out_shape=[jax.ShapeDtypeStruct(*o) for o in outs],...]
  transfers between devices with their start and end apart: 4 -> 4, of which waited for: 2 -> 2; matrix products, arithmetic and copies ran while one was open for 0% -> 0% of each run, Pallas kernels for 11% -> 12%
where the time goes in v5:
time: 32.4 us; the launch traced here: 32.2 us
  starting transfers between devices  14.6 us (45%)
  Pallas kernels  12.5 us (39%)
  waiting for transfers between devices  4.31 us (13%)
  between operations  0.74 us (2%)
    pallas_call x7, Pallas kernels, kernel(): pl.pallas_call(body, out_shape=[jax.ShapeDtypeStruct(*o) for o in outs],...  12.5 us
    ppermute x1, starting transfers between devices, per_device(): other_t = lax.ppermute(transitions, 'state', partner)  8.88 us
    ppermute x1, waiting for transfers between devices, per_device(): lax.ppermute(pack, ('tm', 'state'), pairs + [(b, a) for a, b in pairs])  2.94 us
    ppermute x1, starting transfers between devices, per_device(): lax.ppermute(pack, ('tm', 'state'), pairs + [(b, a) for a, b in pairs])  1.92 us
    ppermute x1, starting transfers between devices, per_device(): pair = lax.ppermute(scored, 'state', partner)  1.92 us
    ppermute x1, starting transfers between devices, per_device(): out_other = lax.ppermute(out, 'state', partner)  1.92 us
    ppermute x1, waiting for transfers between devices, per_device(): out_other = lax.ppermute(out, 'state', partner)  1.36 us
  transfers between devices with their start and end apart: 4, of which 2 were waited for; matrix products, arithmetic and copies ran while one was open for 0% of the time, Pallas kernels for 12%

profile of v5, /device:TPU:1, one launch (start us, length us, event | category | flops | bytes accessed | tf_op | source)
XLA Modules:
  0.0 32.2 jit_solution(12343803008987021052)
XLA Ops:
  0.6 0.0 copy-start
  0.6 8.9 %collective-permute-start.2 = (bf16[512,1024]{1,0:T(8,128)(2,1)}, bf16[512,1024]{1,0:T(8,128)(2,1)S(1)}, u32[]{:S(2)}, u32[]{:S(2)}) collective-permute-start(bf16[512,1024]{1,0:T(8,128)(2,1)} %own_t.1), channel_id=1, source_target_pairs={{0,1},{1,0},{2,3},{3,2},{4,5},{5,4},{6,7},{7,6},{8,9},{9,8},{10,11... | collective-permute-start | bytes 3145736 | tf_op jit(solution)/shard_map/ppermute | solution.py:365
  9.5 2.8 %shard_map.77 = (bf16[64,1664]{1,0:T(8,128)(2,1)S(1)}, f32[4,72,128]{2,1,0:T(8,128)S(1)}, bf16[1024,1024]{1,0:T(8,128)(2,1)S(1)}, f32[8,512]{1,0:T(8,128)S(1)}) custom-call(f32[64,512]{1,0:T(8,128)} %bitcast.1, f32[512,512]{1,0:T(8,128)} %means.1, f32[512,512]{1,0:T(8,128)} %precs.1, s32[4,16]{1,0:T(4,128)} %flags.1, bf16[512]{0:T(512)(128)(2,1)} %init.1), custom_call_target="tpu_custom_call" | custom-call | flops 1000000000 | bytes 1048576 | tf_op jit(solution)/shard_map/pallas_call | solution.py:323
  12.3 1.9 %collective-permute-start = (bf16[64,1664]{1,0:T(8,128)(2,1)S(1)}, bf16[64,1664]{1,0:T(8,128)(2,1)S(1)}, u32[]{:S(2)}, u32[]{:S(2)}) collective-permute-start(bf16[64,1664]{1,0:T(8,128)(2,1)S(1)} %get-tuple-element.10.own_pack), channel_id=1, source_target_pairs={{1,2},{3,4},{5,6},{7,8},{9,10},{11,12},{13,14},{15,16},{17,18},{19... | collective-permute-start | bytes 638984 | tf_op jit(solution)/shard_map/ppermute | solution.py:364
  14.2 1.9 %collective-permute-start.1 = (f32[4,72,128]{2,1,0:T(8,128)S(1)}, f32[4,72,128]{2,1,0:T(8,128)S(1)}, u32[]{:S(2)}, u32[]{:S(2)}) collective-permute-start(f32[4,72,128]{2,1,0:T(8,128)S(1)} %get-tuple-element.9.own_scores), channel_id=1, source_target_pairs={{0,1},{1,0},{2,3},{3,2},{4,5},{5,4},{6,7},{7,6},{8,9},{9,8},{10,11... | collective-permute-start | bytes 442376 | tf_op jit(solution)/shard_map/ppermute | solution.py:366
  16.2 0.0 copy-done
  16.2 0.3 %shard_map.80.own_turned = bf16[512,1024]{1,0:T(8,128)(2,1)S(1)} custom-call(bf16[512,1024]{1,0:T(8,128)(2,1)S(1)} %copy-done), custom_call_target="tpu_custom_call" | custom-call | flops 1000000000 | bytes 1048576 | tf_op jit(solution)/shard_map/pallas_call | solution.py:323
  16.5 2.9 %collective-permute-done.halo_pack = bf16[64,1664]{1,0:T(8,128)(2,1)S(1)} collective-permute-done((bf16[64,1664]{1,0:T(8,128)(2,1)S(1)}, bf16[64,1664]{1,0:T(8,128)(2,1)S(1)}, u32[]{:S(2)}, u32[]{:S(2)}) %collective-permute-start) | collective-permute-done | bytes 213024 | tf_op jit(solution)/shard_map/ppermute | solution.py:364
  19.5 0.5 %shard_map.78 = (f32[4,64,128]{2,1,0:T(8,128)S(1)}, f32[4,64,128]{2,1,0:T(8,128)S(1)}, f32[128,128]{1,0:T(8,128)S(1)}) custom-call(bf16[64,1664]{1,0:T(8,128)(2,1)S(1)} %get-tuple-element.10.own_pack, bf16[64,1664]{1,0:T(8,128)(2,1)S(1)} %collective-permute-done.halo_pack, bf16[1024,1024]{1,0:T(8,128)(2,1)S(1)} %get-tuple-element.11.w, ...), custom_call_target="tpu_custom_call" | custom-call | flops 1000000000 | bytes 1048576 | tf_op jit(solution)/shard_map/pallas_call | solution.py:323
  19.9 0.0 collective-permute-done.1.pair_scores
  20.0 0.3 shard_map.79.emission
  20.3 0.0 collective-permute-done.2.source.other_t
  20.3 0.3 %shard_map.81.other_turned = bf16[512,1024]{1,0:T(8,128)(2,1)S(1)} custom-call(bf16[512,1024]{1,0:T(8,128)(2,1)S(1)} %collective-permute-done.2.source.other_t), custom_call_target="tpu_custom_call" | custom-call | flops 1000000000 | bytes 1048576 | tf_op jit(solution)/shard_map/pallas_call | solution.py:323
  20.6 7.5 %shard_map.82.own = bf16[64,1280]{1,0:T(8,128)(2,1)S(1)} custom-call(f32[128,1024]{1,0:T(8,128)S(1)} %shard_map.79.emission, f32[128,128]{1,0:T(8,128)S(1)} %get-tuple-element.15.place, f32[4,72,128]{2,1,0:T(8,128)S(1)} %get-tuple-element.9.own_scores, f32[4,72,128]{2,1,0:T(8,128)S(1)} %collective-permute-done.1.pair_scores, bf16[512,1024]{1,0:T(8,128)(2,1)S(1)} %copy-done, ...), custom_call_target="tpu_custom_call" | custom-call | flops 10000000000 | bytes 1048576 | tf_op jit(solution)/shard_map/pallas_call | solution.py:323
  28.1 1.9 %collective-permute-start.3 = (bf16[64,1280]{1,0:T(8,128)(2,1)S(1)}, bf16[64,1280]{1,0:T(8,128)(2,1)S(1)}, u32[]{:S(2)}, u32[]{:S(2)}) collective-permute-start(bf16[64,1280]{1,0:T(8,128)(2,1)S(1)} %shard_map.82.own), channel_id=1, source_target_pairs={{0,1},{1,0},{2,3},{3,2},{4,5},{5,4},{6,7},{7,6},{8,9},{9,8},{10,11... | collective-permute-start | bytes 491528 | tf_op jit(solution)/shard_map/ppermute | solution.py:392
  30.0 1.4 %collective-permute-done.3.other = bf16[64,1280]{1,0:T(8,128)(2,1)S(1)} collective-permute-done((bf16[64,1280]{1,0:T(8,128)(2,1)S(1)}, bf16[64,1280]{1,0:T(8,128)(2,1)S(1)}, u32[]{:S(2)}, u32[]{:S(2)}) %collective-permute-start.3) | collective-permute-done | bytes 163872 | tf_op jit(solution)/shard_map/ppermute | solution.py:392
  31.4 0.8 %shard_map.83 = (bf16[4,16,512]{2,1,0:T(8,128)(2,1)}, f32[4,8]{1,0:T(4,128)}) custom-call(bf16[64,1280]{1,0:T(8,128)(2,1)S(1)} %shard_map.82.own, bf16[64,1280]{1,0:T(8,128)(2,1)S(1)} %collective-permute-done.3.other), custom_call_target="tpu_custom_call" | custom-call | flops 1000000 | bytes 1048576 | tf_op jit(solution)/shard_map/pallas_call | solution.py:323
Async XLA Ops:
  0.6 15.5 %copy-start = (bf16[512,1024]{1,0:T(8,128)(2,1)S(1)}, bf16[512,1024]{1,0:T(8,128)(2,1)}, u32[]{:S(2)}) copy-start(bf16[512,1024]{1,0:T(8,128)(2,1)} %own_t.1) | copy-start | bytes 3145732
  0.6 19.6 %collective-permute-start.2 = (bf16[512,1024]{1,0:T(8,128)(2,1)}, bf16[512,1024]{1,0:T(8,128)(2,1)S(1)}, u32[]{:S(2)}, u32[]{:S(2)}) collective-permute-start(bf16[512,1024]{1,0:T(8,128)(2,1)} %own_t.1), channel_id=1, source_target_pairs={{0,1},{1,0},{2,3},{3,2},{4,5},{5,4},{6,7},{7,6},{8,9},{9,8},{10,11... | collective-permute-start | bytes 3145736 | tf_op jit(solution)/shard_map/ppermute | solution.py:365
  12.3 7.2 %collective-permute-start = (bf16[64,1664]{1,0:T(8,128)(2,1)S(1)}, bf16[64,1664]{1,0:T(8,128)(2,1)S(1)}, u32[]{:S(2)}, u32[]{:S(2)}) collective-permute-start(bf16[64,1664]{1,0:T(8,128)(2,1)S(1)} %get-tuple-element.10.own_pack), channel_id=1, source_target_pairs={{1,2},{3,4},{5,6},{7,8},{9,10},{11,12},{13,14},{15,16},{17,18},{19... | collective-permute-start | bytes 638984 | tf_op jit(solution)/shard_map/ppermute | solution.py:364
  14.2 5.7 %collective-permute-start.1 = (f32[4,72,128]{2,1,0:T(8,128)S(1)}, f32[4,72,128]{2,1,0:T(8,128)S(1)}, u32[]{:S(2)}, u32[]{:S(2)}) collective-permute-start(f32[4,72,128]{2,1,0:T(8,128)S(1)} %get-tuple-element.9.own_scores), channel_id=1, source_target_pairs={{0,1},{1,0},{2,3},{3,2},{4,5},{5,4},{6,7},{7,6},{8,9},{9,8},{10,11... | collective-permute-start | bytes 442376 | tf_op jit(solution)/shard_map/ppermute | solution.py:366
  28.1 3.3 %collective-permute-start.3 = (bf16[64,1280]{1,0:T(8,128)(2,1)S(1)}, bf16[64,1280]{1,0:T(8,128)(2,1)S(1)}, u32[]{:S(2)}, u32[]{:S(2)}) collective-permute-start(bf16[64,1280]{1,0:T(8,128)(2,1)S(1)} %shard_map.82.own), channel_id=1, source_target_pairs={{0,1},{1,0},{2,3},{3,2},{4,5},{5,4},{6,7},{7,6},{8,9},{9,8},{10,11... | collective-permute-start | bytes 491528 | tf_op jit(solution)/shard_map/ppermute | solution.py:392

commit v6 on v5

--- a/solution.py
+++ b/solution.py
@@ -10,7 +10,7 @@
 acoustic = 0.1
 VMEM = pltpu.VMEM
 MIB = 1 << 20
-UNROLL = 3
+UNROLL = 15
 PARTS = 2
 SCALE = 2.0**108
 TRANSPOSED = (((1,), (1,)), ((), ()))
@@ -44,21 +44,14 @@
     rows = feats.shape[0]
     streams, frames = flags.shape
     pieces = width // 128
-    pairs = [(feats, x_in)]
+    pairs = [(feats, x_in), (flags, flag_in), (init, init_in)]
     for n in range(PARTS):
         at = slice(n * half // PARTS, (n + 1) * half // PARTS)
         pairs += [(precs.at[at], prec_in.at[at]), (means.at[at], mean_in.at[at])]
-    pairs += [(flags, flag_in), (init, init_in)]
     copies = [pltpu.make_async_copy(*p, sems.at[n]) for n, p in enumerate(pairs)]
     for copy in copies:
         copy.start()
-    for n in (0, -2, -1):
-        copies[n].wait()
-    init_row = init_in[...].astype(f32).reshape(1, half)
-    for c in range(half // 128):
-        scored[c, rows : rows + 8, :] = jnp.broadcast_to(
-            init_row[:, 128 * c : 128 * c + 128], (8, 128)
-        )
+    copies[0].wait()
     x_hi, x_lo = split_pair(acoustic * x_in[...])
     pack[:, 0:width] = x_hi
     pack[:, width : 2 * width] = x_lo
@@ -96,10 +89,18 @@
 
     tiles = half // 128
     for part in range(PARTS):
-        copies[1 + 2 * part].wait()
-        copies[2 + 2 * part].wait()
+        copies[3 + 2 * part].wait()
+        copies[4 + 2 * part].wait()
         for n in range(part * tiles // PARTS, (part + 1) * tiles // PARTS):
             score(n, *prepare(n))
+
+    copies[1].wait()
+    copies[2].wait()
+    init_row = init_in[...].astype(f32).reshape(1, half)
+    for c in range(half // 128):
+        scored[c, rows : rows + 8, :] = jnp.broadcast_to(
+            init_row[:, 128 * c : 128 * c + 128], (8, 128)
+        )
 
     top = scored[0, 0:rows, :]
     for c in range(1, tiles):

time: 32.4 us -> 32.1 us (level)
  no operation moved by 1% of the time
where the time goes in v6:
time: 32.1 us; the launch traced here: 31.9 us
  starting transfers between devices  14.6 us (45%)
  Pallas kernels  12.2 us (38%)
  waiting for transfers between devices  4.31 us (13%)
  between operations  0.74 us (2%)
    pallas_call x7, Pallas kernels, kernel(): pl.pallas_call(body, out_shape=[jax.ShapeDtypeStruct(*o) for o in outs],...  12.2 us
    ppermute x1, starting transfers between devices, per_device(): other_t = lax.ppermute(transitions, 'state', partner)  8.88 us
    ppermute x1, waiting for transfers between devices, per_device(): lax.ppermute(pack, ('tm', 'state'), pairs + [(b, a) for a, b in pairs])  2.94 us
    ppermute x1, starting transfers between devices, per_device(): lax.ppermute(pack, ('tm', 'state'), pairs + [(b, a) for a, b in pairs])  1.92 us
    ppermute x1, starting transfers between devices, per_device(): pair = lax.ppermute(scored, 'state', partner)  1.92 us
    ppermute x1, starting transfers between devices, per_device(): out_other = lax.ppermute(out, 'state', partner)  1.92 us
    ppermute x1, waiting for transfers between devices, per_device(): out_other = lax.ppermute(out, 'state', partner)  1.36 us
  transfers between devices with their start and end apart: 4, of which 2 were waited for; matrix products, arithmetic and copies ran while one was open for 0% of the time, Pallas kernels for 12%

profile of v6, /device:TPU:1, one launch (start us, length us, event | category | flops | bytes accessed | tf_op | source)
XLA Modules:
  0.0 31.9 jit_solution(13189708129362722958)
XLA Ops:
  0.6 0.0 copy-start
  0.6 8.9 %collective-permute-start.2 = (bf16[512,1024]{1,0:T(8,128)(2,1)}, bf16[512,1024]{1,0:T(8,128)(2,1)S(1)}, u32[]{:S(2)}, u32[]{:S(2)}) collective-permute-start(bf16[512,1024]{1,0:T(8,128)(2,1)} %own_t.1), channel_id=1, source_target_pairs={{0,1},{1,0},{2,3},{3,2},{4,5},{5,4},{6,7},{7,6},{8,9},{9,8},{10,11... | collective-permute-start | bytes 3145736 | tf_op jit(solution)/shard_map/ppermute | solution.py:366
  9.5 2.6 %shard_map.77 = (bf16[64,1664]{1,0:T(8,128)(2,1)S(1)}, f32[4,72,128]{2,1,0:T(8,128)S(1)}, bf16[1024,1024]{1,0:T(8,128)(2,1)S(1)}, f32[8,512]{1,0:T(8,128)S(1)}) custom-call(f32[64,512]{1,0:T(8,128)} %bitcast.1, f32[512,512]{1,0:T(8,128)} %means.1, f32[512,512]{1,0:T(8,128)} %precs.1, s32[4,16]{1,0:T(4,128)} %flags.1, bf16[512]{0:T(512)(128)(2,1)} %init.1), custom_call_target="tpu_custom_call" | custom-call | flops 1000000000 | bytes 1048576 | tf_op jit(solution)/shard_map/pallas_call | solution.py:324
  12.2 1.9 %collective-permute-start = (bf16[64,1664]{1,0:T(8,128)(2,1)S(1)}, bf16[64,1664]{1,0:T(8,128)(2,1)S(1)}, u32[]{:S(2)}, u32[]{:S(2)}) collective-permute-start(bf16[64,1664]{1,0:T(8,128)(2,1)S(1)} %get-tuple-element.10.own_pack), channel_id=1, source_target_pairs={{1,2},{3,4},{5,6},{7,8},{9,10},{11,12},{13,14},{15,16},{17,18},{19... | collective-permute-start | bytes 638984 | tf_op jit(solution)/shard_map/ppermute | solution.py:365
  14.1 1.9 %collective-permute-start.1 = (f32[4,72,128]{2,1,0:T(8,128)S(1)}, f32[4,72,128]{2,1,0:T(8,128)S(1)}, u32[]{:S(2)}, u32[]{:S(2)}) collective-permute-start(f32[4,72,128]{2,1,0:T(8,128)S(1)} %get-tuple-element.9.own_scores), channel_id=1, source_target_pairs={{0,1},{1,0},{2,3},{3,2},{4,5},{5,4},{6,7},{7,6},{8,9},{9,8},{10,11... | collective-permute-start | bytes 442376 | tf_op jit(solution)/shard_map/ppermute | solution.py:367
  16.0 0.0 copy-done
  16.0 0.3 %shard_map.80.own_turned = bf16[512,1024]{1,0:T(8,128)(2,1)S(1)} custom-call(bf16[512,1024]{1,0:T(8,128)(2,1)S(1)} %copy-done), custom_call_target="tpu_custom_call" | custom-call | flops 1000000000 | bytes 1048576 | tf_op jit(solution)/shard_map/pallas_call | solution.py:324
  16.4 2.9 %collective-permute-done.halo_pack = bf16[64,1664]{1,0:T(8,128)(2,1)S(1)} collective-permute-done((bf16[64,1664]{1,0:T(8,128)(2,1)S(1)}, bf16[64,1664]{1,0:T(8,128)(2,1)S(1)}, u32[]{:S(2)}, u32[]{:S(2)}) %collective-permute-start) | collective-permute-done | bytes 213024 | tf_op jit(solution)/shard_map/ppermute | solution.py:365
  19.3 0.5 %shard_map.78 = (f32[4,64,128]{2,1,0:T(8,128)S(1)}, f32[4,64,128]{2,1,0:T(8,128)S(1)}, f32[128,128]{1,0:T(8,128)S(1)}) custom-call(bf16[64,1664]{1,0:T(8,128)(2,1)S(1)} %get-tuple-element.10.own_pack, bf16[64,1664]{1,0:T(8,128)(2,1)S(1)} %collective-permute-done.halo_pack, bf16[1024,1024]{1,0:T(8,128)(2,1)S(1)} %get-tuple-element.11.w, ...), custom_call_target="tpu_custom_call" | custom-call | flops 1000000000 | bytes 1048576 | tf_op jit(solution)/shard_map/pallas_call | solution.py:324
  19.8 0.0 collective-permute-done.1.pair_scores
  19.8 0.3 shard_map.79.emission
  20.1 0.0 collective-permute-done.2.source.other_t
  20.1 0.3 %shard_map.81.other_turned = bf16[512,1024]{1,0:T(8,128)(2,1)S(1)} custom-call(bf16[512,1024]{1,0:T(8,128)(2,1)S(1)} %collective-permute-done.2.source.other_t), custom_call_target="tpu_custom_call" | custom-call | flops 1000000000 | bytes 1048576 | tf_op jit(solution)/shard_map/pallas_call | solution.py:324
  20.5 7.4 %shard_map.82.own = bf16[64,1280]{1,0:T(8,128)(2,1)S(1)} custom-call(f32[128,1024]{1,0:T(8,128)S(1)} %shard_map.79.emission, f32[128,128]{1,0:T(8,128)S(1)} %get-tuple-element.15.place, f32[4,72,128]{2,1,0:T(8,128)S(1)} %get-tuple-element.9.own_scores, f32[4,72,128]{2,1,0:T(8,128)S(1)} %collective-permute-done.1.pair_scores, bf16[512,1024]{1,0:T(8,128)(2,1)S(1)} %copy-done, ...), custom_call_target="tpu_custom_call" | custom-call | flops 10000000000 | bytes 1048576 | tf_op jit(solution)/shard_map/pallas_call | solution.py:324
  27.9 1.9 %collective-permute-start.3 = (bf16[64,1280]{1,0:T(8,128)(2,1)S(1)}, bf16[64,1280]{1,0:T(8,128)(2,1)S(1)}, u32[]{:S(2)}, u32[]{:S(2)}) collective-permute-start(bf16[64,1280]{1,0:T(8,128)(2,1)S(1)} %shard_map.82.own), channel_id=1, source_target_pairs={{0,1},{1,0},{2,3},{3,2},{4,5},{5,4},{6,7},{7,6},{8,9},{9,8},{10,11... | collective-permute-start | bytes 491528 | tf_op jit(solution)/shard_map/ppermute | solution.py:393
  29.8 1.4 %collective-permute-done.3.other = bf16[64,1280]{1,0:T(8,128)(2,1)S(1)} collective-permute-done((bf16[64,1280]{1,0:T(8,128)(2,1)S(1)}, bf16[64,1280]{1,0:T(8,128)(2,1)S(1)}, u32[]{:S(2)}, u32[]{:S(2)}) %collective-permute-start.3) | collective-permute-done | bytes 163872 | tf_op jit(solution)/shard_map/ppermute | solution.py:393
  31.1 0.8 %shard_map.83 = (bf16[4,16,512]{2,1,0:T(8,128)(2,1)}, f32[4,8]{1,0:T(4,128)}) custom-call(bf16[64,1280]{1,0:T(8,128)(2,1)S(1)} %shard_map.82.own, bf16[64,1280]{1,0:T(8,128)(2,1)S(1)} %collective-permute-done.3.other), custom_call_target="tpu_custom_call" | custom-call | flops 1000000 | bytes 1048576 | tf_op jit(solution)/shard_map/pallas_call | solution.py:324
Async XLA Ops:
  0.6 15.4 %copy-start = (bf16[512,1024]{1,0:T(8,128)(2,1)S(1)}, bf16[512,1024]{1,0:T(8,128)(2,1)}, u32[]{:S(2)}) copy-start(bf16[512,1024]{1,0:T(8,128)(2,1)} %own_t.1) | copy-start | bytes 3145732
  0.6 19.5 %collective-permute-start.2 = (bf16[512,1024]{1,0:T(8,128)(2,1)}, bf16[512,1024]{1,0:T(8,128)(2,1)S(1)}, u32[]{:S(2)}, u32[]{:S(2)}) collective-permute-start(bf16[512,1024]{1,0:T(8,128)(2,1)} %own_t.1), channel_id=1, source_target_pairs={{0,1},{1,0},{2,3},{3,2},{4,5},{5,4},{6,7},{7,6},{8,9},{9,8},{10,11... | collective-permute-start | bytes 3145736 | tf_op jit(solution)/shard_map/ppermute | solution.py:366
  12.2 7.2 %collective-permute-start = (bf16[64,1664]{1,0:T(8,128)(2,1)S(1)}, bf16[64,1664]{1,0:T(8,128)(2,1)S(1)}, u32[]{:S(2)}, u32[]{:S(2)}) collective-permute-start(bf16[64,1664]{1,0:T(8,128)(2,1)S(1)} %get-tuple-element.10.own_pack), channel_id=1, source_target_pairs={{1,2},{3,4},{5,6},{7,8},{9,10},{11,12},{13,14},{15,16},{17,18},{19... | collective-permute-start | bytes 638984 | tf_op jit(solution)/shard_map/ppermute | solution.py:365
  14.1 5.7 %collective-permute-start.1 = (f32[4,72,128]{2,1,0:T(8,128)S(1)}, f32[4,72,128]{2,1,0:T(8,128)S(1)}, u32[]{:S(2)}, u32[]{:S(2)}) collective-permute-start(f32[4,72,128]{2,1,0:T(8,128)S(1)} %get-tuple-element.9.own_scores), channel_id=1, source_target_pairs={{0,1},{1,0},{2,3},{3,2},{4,5},{5,4},{6,7},{7,6},{8,9},{9,8},{10,11... | collective-permute-start | bytes 442376 | tf_op jit(solution)/shard_map/ppermute | solution.py:367
  27.9 3.3 %collective-permute-start.3 = (bf16[64,1280]{1,0:T(8,128)(2,1)S(1)}, bf16[64,1280]{1,0:T(8,128)(2,1)S(1)}, u32[]{:S(2)}, u32[]{:S(2)}) collective-permute-start(bf16[64,1280]{1,0:T(8,128)(2,1)S(1)} %shard_map.82.own), channel_id=1, source_target_pairs={{0,1},{1,0},{2,3},{3,2},{4,5},{5,4},{6,7},{7,6},{8,9},{9,8},{10,11... | collective-permute-start | bytes 491528 | tf_op jit(solution)/shard_map/ppermute | solution.py:393
